TPU v7x, 256 devices: a whole 4x4x8 slice. The times are simulated.
256 devices in a mesh: edge: 64 (over x, z, core), feat: 4 (over y).
Axes of the slice: x: 4, y: 4, z: 8, core: 2. Of those that a mesh axis runs over, the one named last changes fastest.
Arguments:
- node_feat: bfloat16 [131072, 128], P('edge'), may hold values from -6 to 6
- cotangent: bfloat16 [131072, 128], P('edge'), may hold values from -6 to 6
- w_msg: bfloat16 [128, 128], replicated, may hold values from -0.5 to 0.5
- w_self: bfloat16 [128, 128], replicated, may hold values from -0.5 to 0.5
- adjacency: bfloat16 [64, 4, 64, 128, 128], P('edge', 'feat'), may hold values from -0.125 to 0.125
- edge_src: int32 [64, 4, 64], P('edge', 'feat'), may hold values from 0 to 127
- edge_dst: int32 [64, 4, 64], P('edge', 'feat'), may hold values from 0 to 127
- send_src: int32 [64, 4, 64, 2], P('edge', 'feat'), may hold values from 0 to 15
- recv_dst: int32 [64, 4, 64, 2], P('edge', 'feat'), may hold values from 0 to 15
- live: int32 [64, 4], P('edge', 'feat'), may hold values from 4 to 64, as said below
Outputs:
- out_feat: bfloat16 [131072, 128], P('edge')
- grad_feat: bfloat16 [131072, 128], P('edge')
- grad_wmsg: float32 [128, 128], replicated
- grad_wself: float32 [128, 128], replicated
Inputs may be any that keep to these rules, and one draw needn't show every extreme that they name: Each device has between 64 // 16 (at least 1) and 64 live blocks; one device always has all 64 live.
All inputs are finite; a program needn't handle non-finite values.
Results may differ from a plain program's by a relative error of at most 0.0054.
Values may be sent and summed in bfloat16 or wider, within the bound.
A program may use at most 128 MiB of HBM per device.

v0:
```python
import math

import jax
import jax.numpy as jnp
from jax import lax
from jax.sharding import PartitionSpec as P


def sent_to_all(value, axis):
    peers = lax.axis_size(axis)
    return lax.all_to_all(
        jnp.broadcast_to(value[None], (peers, *value.shape)), axis, 0, 0, tiled=True
    )


def over_copies(value, axis):
    everything = sent_to_all(value, axis)
    return jnp.sum(everything, axis=0)


def over_pieces(value, axis):
    return lax.all_gather(value, axis).sum(0)


def edge_terms(blocks_adj, source_rows, pick_ids, put_ids, slot_count, live_count, forward):
    block_count = blocks_adj.shape[0]
    width = source_rows.shape[-1]
    block_size = blocks_adj.shape[-1]

    def block_terms(blocks, picked):
        if forward:
            return jnp.einsum("eij,ejh->eih", blocks, picked, preferred_element_type=jnp.float32)
        return jnp.einsum("eij,eih->ejh", blocks, picked, preferred_element_type=jnp.float32)

    empty = jnp.zeros((slot_count, block_size, width), jnp.float32)
    group_size = math.gcd(32, block_count)
    round_count = (live_count + group_size - 1) // group_size

    def one_round(turn_index, running):
        offset = turn_index * group_size
        blocks = lax.dynamic_slice_in_dim(blocks_adj, offset, group_size, 0)
        picks = lax.dynamic_slice_in_dim(pick_ids, offset, group_size, 0)
        puts = lax.dynamic_slice_in_dim(put_ids, offset, group_size, 0)
        keep_mask = (offset + jnp.arange(group_size, dtype=jnp.int32) < live_count).astype(
            jnp.float32
        )
        terms = block_terms(blocks, jnp.take(source_rows, picks, axis=0)) * keep_mask[:, None, None]
        return running.at[puts].add(terms)

    return lax.fori_loop(0, round_count, one_round, empty)


def body(
    node_feat, cotangent, w_msg, w_self, adjacency, edge_src, edge_dst, send_src, recv_dst, live
):
    block_size = adjacency.shape[-1]
    hidden = node_feat.shape[1]
    owned_blocks = node_feat.shape[0] // block_size
    peer_count = lax.axis_size("edge")
    send_slots = send_src.shape[-1]
    dest_slots = recv_dst.shape[-1]
    send_ids = send_src.reshape(-1)
    recv_ids = recv_dst.reshape(-1)
    blocks_adj = adjacency.reshape(-1, block_size, block_size)
    src_ids = edge_src.reshape(-1)
    dst_ids = edge_dst.reshape(-1)
    live_count = live.reshape(())
    messages = jnp.dot(node_feat, w_msg, preferred_element_type=jnp.float32).astype(jnp.bfloat16)
    outgoing = jnp.take(messages.reshape(owned_blocks, block_size, hidden), send_ids, axis=0)
    incoming = lax.all_to_all(
        outgoing.reshape(peer_count, send_slots, block_size, hidden),
        "edge",
        split_axis=0,
        concat_axis=0,
        tiled=True,
    )
    incoming = incoming.reshape(-1, block_size, hidden)
    partials = edge_terms(
        blocks_adj, incoming, src_ids, dst_ids, peer_count * dest_slots, live_count, True
    )
    returned = lax.all_to_all(
        partials.reshape(peer_count, dest_slots, block_size, hidden),
        "edge",
        split_axis=0,
        concat_axis=0,
        tiled=True,
    )
    owner_sum = (
        jnp.zeros((owned_blocks, block_size, hidden), jnp.float32)
        .at[recv_ids]
        .add(returned.reshape(-1, block_size, hidden))
    )
    aggregate = over_copies(owner_sum, "feat")
    preact = jnp.dot(node_feat, w_self, preferred_element_type=jnp.float32) + aggregate.reshape(
        -1, hidden
    )
    sigmoid_pre = jax.nn.sigmoid(preact)
    out_feat = (preact * sigmoid_pre).astype(jnp.bfloat16)
    grad_pre = (
        cotangent.astype(jnp.float32) * sigmoid_pre * (1.0 + preact * (1.0 - sigmoid_pre))
    ).astype(jnp.bfloat16)
    wself_part = lax.dot_general(
        node_feat, grad_pre, (((0,), (0,)), ((), ())), preferred_element_type=jnp.float32
    )
    grad_out = jnp.take(grad_pre.reshape(owned_blocks, block_size, hidden), recv_ids, axis=0)
    grad_in = lax.all_to_all(
        grad_out.reshape(peer_count, dest_slots, block_size, hidden),
        "edge",
        split_axis=0,
        concat_axis=0,
        tiled=True,
    )
    grad_in = grad_in.reshape(-1, block_size, hidden)
    grad_partials = edge_terms(
        blocks_adj, grad_in, dst_ids, src_ids, peer_count * send_slots, live_count, False
    )
    grad_back = lax.all_to_all(
        grad_partials.reshape(peer_count, send_slots, block_size, hidden),
        "edge",
        split_axis=0,
        concat_axis=0,
        tiled=True,
    )
    grad_owner = (
        jnp.zeros((owned_blocks, block_size, hidden), jnp.float32)
        .at[send_ids]
        .add(grad_back.reshape(-1, block_size, hidden))
    )
    grad_sum = over_copies(grad_owner, "feat")
    grad_msg = grad_sum.reshape(-1, hidden).astype(jnp.bfloat16)
    wmsg_part = lax.dot_general(
        node_feat, grad_msg, (((0,), (0,)), ((), ())), preferred_element_type=jnp.float32
    )
    grad_wmsg, grad_wself = (over_pieces(wmsg_part, "edge"), over_pieces(wself_part, "edge"))
    grad_feat = (
        jnp.dot(grad_pre, w_self.T, preferred_element_type=jnp.float32)
        + jnp.dot(grad_msg, w_msg.T, preferred_element_type=jnp.float32)
    ).astype(jnp.bfloat16)
    return (out_feat, grad_feat, grad_wmsg, grad_wself)


def solution(mesh):
    in_specs = (
        P("edge", None),
        P("edge", None),
        P(),
        P(),
        P("edge", "feat", None, None, None),
        P("edge", "feat", None),
        P("edge", "feat", None),
        P("edge", "feat", None, None),
        P("edge", "feat", None, None),
        P("edge", "feat"),
    )
    out_specs = (P("edge", None), P("edge", None), P(), P())
    return jax.shard_map(body, mesh=mesh, in_specs=in_specs, out_specs=out_specs, check_vma=False)
```

profile of v0, /device:TPU:1, one launch (start us, length us, event | category | flops | bytes accessed | tf_op | source)
XLA Modules:
  0.0 925.1 jit_solution(7644309299755211815)
XLA Ops:
  12.3 4.6 broadcast_select_fusion.1
  16.9 13.2 %all-to-all-start = ((bf16[64,2,128,128]{3,2,1,0:T(8,128)(2,1)}), bf16[64,2,128,128]{3,2,1,0:T(8,128)(2,1)}, u32[]{:S(2)}, u32[]{:S(2)}) async-start(bf16[64,2,128,128]{3,2,1,0:T(8,128)(2,1)} %bitcast.63), calls=%async_computation | async-start | bytes 8388608 | tf_op jit(solution)/shard_map/all_to_all | solution.py:70
  30.8 95.2 %all-to-all-done = bf16[64,2,128,128]{3,2,1,0:T(8,128)(2,1)} async-done(((bf16[64,2,128,128]{3,2,1,0:T(8,128)(2,1)}), bf16[64,2,128,128]{3,2,1,0:T(8,128)(2,1)}, u32[]{:S(2)}, u32[]{:S(2)}) %all-to-all-start) | async-done | bytes 4194336 | tf_op jit(solution)/shard_map/all_to_all | solution.py:70
  126.0 4.3 broadcast.83.clone
  130.2 12.9 %while.20 = (s32[]{:T(128)}, f32[128,128,128]{2,1,0:T(8,128)}, s32[]{:T(128)}, s32[64]{0:T(128)S(1)}, bf16[64,128,128]{2,1,0:T(8,128)(2,1)}, /*index=5*/s32[64]{...) while((s32[]{:T(128)}, f32[128,128,128]{2,1,0:T(8,128)}, ...), condition=%wide.region_2.5_spmd, body=%wide.region_0.4_spmd.sunk | while | flops 135792000 | bytes 12588407 | solution.py:50
  131.0 3.8 gather_fusion
  137.0 6.2 scatter_fusion
  143.2 19.0 %all-to-all-start.1 = ((f32[64,2,128,128]{3,2,1,0:T(8,128)}), f32[64,2,128,128]{3,2,1,0:T(8,128)}, u32[]{:S(2)}, u32[]{:S(2)}) async-start(f32[64,2,128,128]{3,2,1,0:T(8,128)} %bitcast.56), calls=%async_computation.1 | async-start | bytes 16777216 | tf_op jit(solution)/shard_map/all_to_all | solution.py:81
  162.4 185.5 %all-to-all-done.1 = f32[64,2,128,128]{3,2,1,0:T(8,128)} async-done(((f32[64,2,128,128]{3,2,1,0:T(8,128)}), f32[64,2,128,128]{3,2,1,0:T(8,128)}, u32[]{:S(2)}, u32[]{:S(2)}) %all-to-all-start.1) | async-done | bytes 8388640 | tf_op jit(solution)/shard_map/all_to_all | solution.py:81
  348.0 17.0 %scatter_fusion.2 = f32[16,128,128]{2,1,0:T(8,128)S(1)} fusion(f32[16,128,128]{2,1,0:T(8,128)S(1)} %broadcast.80.clone, s32[128]{0:T(128)S(1)} %fusion.13, f32[128,128,128]{2,1,0:T(8,128)} %bitcast.10), kind=kCustom, calls=%fused_computation.6 | custom fusion | flops 2097152 | bytes 25166336 | tf_op jit(solution)/shard_map/scatter-add | solution.py:91
  367.6 4.8 all-to-all-start.2
  372.7 49.2 %all-to-all-done.2 = f32[4,16,128,128]{3,2,1,0:T(8,128)} async-done(((f32[4,16,128,128]{3,2,1,0:T(8,128)}), f32[4,16,128,128]{3,2,1,0:T(8,128)}, u32[]{:S(2)}, u32[]{:S(2)}) %all-to-all-start.2) | async-done | bytes 4194336 | tf_op jit(solution)/shard_map/all_to_all | solution.py:11
  429.0 4.6 broadcast_select_fusion
  433.6 5.6 all-to-all-start.3
  442.1 93.0 %all-to-all-done.3 = bf16[64,2,128,128]{3,2,1,0:T(8,128)(2,1)} async-done(((bf16[64,2,128,128]{3,2,1,0:T(8,128)(2,1)}), bf16[64,2,128,128]{3,2,1,0:T(8,128)(2,1)}, u32[]{:S(2)}, u32[]{:S(2)}) %all-to-all-start.3) | async-done | bytes 4194336 | tf_op jit(solution)/shard_map/all_to_all | solution.py:106
  535.1 4.3 broadcast.83
  539.4 12.9 %while.21 = (s32[]{:T(128)}, f32[128,128,128]{2,1,0:T(8,128)}, s32[]{:T(128)}, s32[64]{0:T(128)S(1)}, bf16[64,128,128]{1,2,0:T(8,128)(2,1)}, /*index=5*/s32[64]{...) while((s32[]{:T(128)}, f32[128,128,128]{2,1,0:T(8,128)}, ...), condition=%wide.region_7.10_spmd, body=%wide.region_5.9_spmd.sunk | while | flops 135792000 | bytes 12588407 | solution.py:50
  540.1 3.8 gather_fusion.1
  546.1 6.2 scatter_fusion.1
  552.3 18.9 %all-to-all-start.4 = ((f32[64,2,128,128]{3,2,1,0:T(8,128)}), f32[64,2,128,128]{3,2,1,0:T(8,128)}, u32[]{:S(2)}, u32[]{:S(2)}) async-start(f32[64,2,128,128]{3,2,1,0:T(8,128)} %bitcast.57), calls=%async_computation.4 | async-start | bytes 16777216 | tf_op jit(solution)/shard_map/all_to_all | solution.py:117
  572.5 196.8 %all-to-all-done.4 = f32[64,2,128,128]{3,2,1,0:T(8,128)} async-done(((f32[64,2,128,128]{3,2,1,0:T(8,128)}), f32[64,2,128,128]{3,2,1,0:T(8,128)}, u32[]{:S(2)}, u32[]{:S(2)}) %all-to-all-start.4) | async-done | bytes 8388640 | tf_op jit(solution)/shard_map/all_to_all | solution.py:117
  769.4 17.0 %scatter_fusion.3 = f32[16,128,128]{2,1,0:T(8,128)S(1)} fusion(f32[16,128,128]{2,1,0:T(8,128)S(1)} %broadcast.80, s32[128]{0:T(128)S(1)} %fusion.14, f32[128,128,128]{2,1,0:T(8,128)} %bitcast.17), kind=kCustom, calls=%fused_computation.7 | custom fusion | flops 2097152 | bytes 25166336 | tf_op jit(solution)/shard_map/scatter-add | solution.py:127
  786.9 52.7 %all_to_all.30 = f32[4,16,128,128]{3,2,1,0:T(8,128)} all-to-all(f32[4,16,128,128]{3,2,1,0:T(8,128)S(1)} %broadcast_in_dim.41), channel_id=1, replica_groups=mesh['edge'=64,'feat'=4] {'feat'}, dimensions={0} | all-to-all | bytes 8388608 | tf_op jit(solution)/shard_map/all_to_all | solution.py:11
  848.9 65.1 %all-gather.5.cloned.1.call-done = f32[8192,128]{0,1:T(8,128)} async-done(((f32[128,128]{0,1:T(8,128)}), f32[8192,128]{0,1:T(8,128)}) %all-gather.5.cloned.1.call-update) | async-done | bytes 4194320 | tf_op jit(solution)/shard_map/all_gather | solution.py:22
  (64 shorter events, 39.2 us)
Async XLA Ops:
  7.2 1.1 copy-start
  16.9 109.0 %all-to-all-start = ((bf16[64,2,128,128]{3,2,1,0:T(8,128)(2,1)}), bf16[64,2,128,128]{3,2,1,0:T(8,128)(2,1)}, u32[]{:S(2)}, u32[]{:S(2)}) async-start(bf16[64,2,128,128]{3,2,1,0:T(8,128)(2,1)} %bitcast.63), calls=%async_computation | async-start | bytes 8388608 | tf_op jit(solution)/shard_map/all_to_all | solution.py:70
  126.0 4.3 copy-start.4
  126.0 4.3 copy-start.5
  143.2 19.0 %copy-start.6 = (s32[1,1,64,2]{2,3,1,0:T(2,128)S(1)}, s32[1,1,64,2]{2,3,1,0:T(2,128)}, u32[]{:S(2)}) copy-start(s32[1,1,64,2]{2,3,1,0:T(2,128)} %param.26) | copy-start | bytes 1540
  143.2 204.7 %all-to-all-start.1 = ((f32[64,2,128,128]{3,2,1,0:T(8,128)}), f32[64,2,128,128]{3,2,1,0:T(8,128)}, u32[]{:S(2)}, u32[]{:S(2)}) async-start(f32[64,2,128,128]{3,2,1,0:T(8,128)} %bitcast.56), calls=%async_computation.1 | async-start | bytes 16777216 | tf_op jit(solution)/shard_map/all_to_all | solution.py:81
  367.6 54.2 %all-to-all-start.2 = ((f32[4,16,128,128]{3,2,1,0:T(8,128)}), f32[4,16,128,128]{3,2,1,0:T(8,128)}, u32[]{:S(2)}, u32[]{:S(2)}) async-start(f32[4,16,128,128]{3,2,1,0:T(8,128)} %broadcast_in_dim.40), calls=%async_computation.2 | async-start | bytes 8388608 | tf_op jit(solution)/shard_map/all_to_all | solution.py:11
  372.4 52.0 %copy-start.3 = (bf16[128,128]{1,0:T(8,128)(2,1)S(1)}, bf16[128,128]{1,0:T(8,128)(2,1)}, u32[]{:S(2)}) copy-start(bf16[128,128]{1,0:T(8,128)(2,1)} %param.21) | copy-start | bytes 98308
  372.5 52.0 %copy-start.7 = (bf16[2048,128]{1,0:T(8,128)(2,1)S(1)}, bf16[2048,128]{1,0:T(8,128)(2,1)}, u32[]{:S(2)}) copy-start(bf16[2048,128]{1,0:T(8,128)(2,1)} %param.19) | copy-start | bytes 1572868
  433.6 5.6 copy-start.1
  433.6 101.5 %all-to-all-start.3 = ((bf16[64,2,128,128]{3,2,1,0:T(8,128)(2,1)}), bf16[64,2,128,128]{3,2,1,0:T(8,128)(2,1)}, u32[]{:S(2)}, u32[]{:S(2)}) async-start(bf16[64,2,128,128]{3,2,1,0:T(8,128)(2,1)} %bitcast.64), calls=%async_computation.3 | async-start | bytes 8388608 | tf_op jit(solution)/shard_map/all_to_all | solution.py:106
  552.3 217.0 %all-to-all-start.4 = ((f32[64,2,128,128]{3,2,1,0:T(8,128)}), f32[64,2,128,128]{3,2,1,0:T(8,128)}, u32[]{:S(2)}, u32[]{:S(2)}) async-start(f32[64,2,128,128]{3,2,1,0:T(8,128)} %bitcast.57), calls=%async_computation.4 | async-start | bytes 16777216 | tf_op jit(solution)/shard_map/all_to_all | solution.py:117
  571.3 272.3 %all-gather.7.cloned.1.call-start = ((), (), s32[]{:S(2)}) async-start(), calls=%async_computation.7 | async-start | bytes 4259840 | tf_op jit(solution)/shard_map/all_gather | solution.py:22
  572.3 341.7 %all-gather.5.cloned.1.call-start = ((), (), s32[]{:S(2)}) async-start(), calls=%async_computation.6 | async-start | bytes 4259840 | tf_op jit(solution)/shard_map/all_gather | solution.py:22
  846.5 1.3 copy-start.2
Sparse Core Ops, SparseCore 0:
  575.2 124.9 all-gather.6
  843.4 70.6 all-gather.4
where the time goes:
time: 927 us; the launch traced here: 925 us
  waiting for transfers between devices  685 us (74%)
  other arithmetic  63.8 us (7%)
  starting transfers between devices  61.6 us (7%)
  blocking collectives  52.7 us (6%)
  local copies, waits for them, and re-layouts  37.4 us (4%)
  between operations  15 us (2%)
  matrix products  9.94 us (1%)
    all_to_all x1, waiting for transfers between devices, body(): lax.all_to_all(grad_partials.reshape(peer_count, send_slots, block_size,...  197 us
    all_to_all x1, waiting for transfers between devices, body(): lax.all_to_all(partials.reshape(peer_count, dest_slots, block_size, hidde...  185 us
    all_to_all x1, waiting for transfers between devices, body(): lax.all_to_all(outgoing.reshape(peer_count, send_slots, block_size, hidde...  95.2 us
    all_to_all x1, waiting for transfers between devices, body(): lax.all_to_all(grad_out.reshape(peer_count, dest_slots, block_size, hidde...  93 us
    all_gather x2, waiting for transfers between devices, over_pieces(): return lax.all_gather(value, axis).sum(0)  65.1 us
    all_to_all x1, blocking collectives, sent_to_all(): lax.all_to_all(jnp.broadcast_to(value[None], (peers, *value.shape)), axis...  52.7 us
    all_to_all x1, waiting for transfers between devices, sent_to_all(): lax.all_to_all(jnp.broadcast_to(value[None], (peers, *value.shape)), axis...  49.2 us
    all_to_all x1, starting transfers between devices, body(): lax.all_to_all(partials.reshape(peer_count, dest_slots, block_size, hidde...  19 us
  transfers between devices with their start and end apart: 7, of which 6 were waited for; matrix products, arithmetic and copies ran while one was open for 3% of the time, Pallas kernels for 0%

commit v1 on v0

v1 whole, which is shorter than its diff:
```python
import jax
import jax.numpy as jnp
from jax import lax
from jax.experimental import pallas as pl
from jax.experimental.pallas import tpu as pltpu
from jax.sharding import PartitionSpec as P

MESH = pl.DeviceIdType.MESH
NX, NY, NZ = 4, 4, 8
BLK = 128
OWN = 16
QTR = OWN // NY
PEERS = 2 * NX
VMEM_LIMIT = 60 * 1024 * 1024
BF16, F32, I32 = jnp.bfloat16, jnp.float32, jnp.int32


def place():
    edge = lax.axis_index("edge")
    y = lax.axis_index("feat")
    return edge // 16, y, (edge // 2) % NZ, edge % 2


def device(x, y, z, c):
    return ((x * NZ + z) * 2 + c, y)


def zoff(k):
    return ((2 * (k % 2) - 1) * ((k + 1) // 2) + NZ) % NZ


def greet(peers):
    barrier = pltpu.get_barrier_semaphore()
    for peer in peers:
        pl.semaphore_signal(barrier, inc=1, device_id=peer, device_id_type=MESH)
    pl.semaphore_wait(barrier, len(peers))


def remote(src, dst, send, recv, peer):
    return pltpu.make_async_remote_copy(
        src_ref=src, dst_ref=dst, send_sem=send, recv_sem=recv, device_id=peer, device_id_type=MESH
    )


def slab_peer(x, c, j):
    return (x + j // 2) % NX, (c + j) % 2


def slab_source(x, c, j):
    return (x + NX - j // 2) % NX, (c + j) % 2


def group_peers(x, y, z, c):
    peers = [device(x, y, (z + d) % NZ, c) for d in range(1, NZ)]
    peers += [device(x, (y + d) % NY, z, c) for d in range(1, NY)]
    for j in range(1, PEERS):
        px, pc = slab_peer(x, c, j)
        peers.append(device(px, y, z, pc))
    return peers


def gather_kernel(tab, q_ref, r_ref, dense, chunk, staged, ls, zs, zr, ys, yr, xs, xr):
    x, y, z, c = place()
    me = x * 2 + c
    greet(group_peers(x, y, z, c))

    def zcopy(d):
        return remote(
            q_ref, dense.at[z, pl.ds(QTR * y, QTR)], zs.at[d], zr.at[d],
            device(x, y, (z + d) % NZ, c),
        )

    def ycopy(k, zi, d):
        quarter = dense.at[zi, pl.ds(QTR * y, QTR)]
        return remote(quarter, quarter, ys.at[k, d], yr.at[k, d], device(x, (y + d) % NY, z, c))

    def xcopy(k, zi, j):
        px, pc = slab_peer(x, c, j)
        return remote(
            staged.at[px * 2 + pc, zi], r_ref.at[me, zi], xs.at[k, j], xr.at[k, j],
            device(px, y, z, pc),
        )

    def spread(k):
        d = zoff(k)
        zi = (z + NZ - d) % NZ

        @pl.when(k > 0)
        def _():
            remote(
                q_ref, dense.at[zi, pl.ds(QTR * y, QTR)], zs.at[d], zr.at[d],
                device(x, y, (z + d) % NZ, c),
            ).wait_recv()

        for dy in (1, 3, 2):
            ycopy(k, zi, dy).start()

    def deliver(k):
        zi = (z + NZ - zoff(k)) % NZ
        for dy in (1, 3, 2):
            part = dense.at[zi, pl.ds(QTR * ((y + NY - dy) % NY), QTR)]
            remote(part, part, ys.at[k, dy], yr.at[k, dy], device(x, y, z, c)).wait_recv()

        chunk[...] = dense[zi]

        def pick(j, carry):
            px, pc = slab_peer(x, c, j)
            pid = px * 2 + pc
            for s in range(2):
                staged[pid, zi, s] = chunk[tab[(zi * PEERS + pid) * 2 + s]]
            return carry

        lax.fori_loop(1, PEERS, pick, 0)
        for s in range(2):
            r_ref[me, zi, s] = chunk[tab[(zi * PEERS + me) * 2 + s]]

        def push(j, carry):
            xcopy(k, zi, j).start()
            return carry

        lax.fori_loop(1, PEERS, push, 0)

    own = pltpu.make_async_copy(q_ref, dense.at[z, pl.ds(QTR * y, QTR)], ls)
    own.start()
    for d in (1, 7, 2, 6, 3, 5, 4):
        zcopy(d).start()
    own.wait()
    spread(0)
    spread(1)

    def step(k, carry):
        @pl.when(k < NZ - 2)
        def _():
            spread(k + 2)

        deliver(k)
        return carry

    lax.fori_loop(0, NZ, step, 0)

    for d in range(1, NZ):
        zcopy(d).wait_send()

    def finish(k, carry):
        zi = (z + NZ - zoff(k)) % NZ
        for dy in range(1, NY):
            ycopy(k, zi, dy).wait_send()

        def each(j, carry):
            xcopy(k, zi, j).wait_send()
            sx, sc = slab_source(x, c, j)
            remote(
                staged.at[me, zi], r_ref.at[sx * 2 + sc, zi], xs.at[k, j], xr.at[k, j],
                device(sx, y, z, sc),
            ).wait_recv()
            return carry

        lax.fori_loop(1, PEERS, each, 0)
        return carry

    lax.fori_loop(0, NZ, finish, 0)


def gather_blocks(tab, quarter):
    dma = pltpu.SemaphoreType.DMA
    return pl.pallas_call(
        gather_kernel,
        name="gather_blocks",
        out_shape=jax.ShapeDtypeStruct((PEERS, NZ, 2, BLK, BLK), BF16),
        in_specs=[
            pl.BlockSpec(memory_space=pltpu.SMEM),
            pl.BlockSpec(memory_space=pltpu.VMEM),
        ],
        out_specs=pl.BlockSpec(memory_space=pltpu.VMEM),
        scratch_shapes=[
            pltpu.VMEM((NZ, OWN, BLK, BLK), BF16),
            pltpu.VMEM((OWN, BLK, BLK), BF16),
            pltpu.VMEM((PEERS, NZ, 2, BLK, BLK), BF16),
            dma,
            dma((NZ,)),
            dma((NZ,)),
            dma((NZ, NY)),
            dma((NZ, NY)),
            dma((NZ, PEERS)),
            dma((NZ, PEERS)),
        ],
        compiler_params=pltpu.CompilerParams(
            collective_id=0, has_side_effects=True, vmem_limit_bytes=VMEM_LIMIT
        ),
    )(tab, quarter)


def scatter_kernel(
    order, keep, last, has, p_ref, o_ref,
    arrived, chunk, runs, ysend, yown, yrecv, zsend, zrecv, ls, xs, xr, ys, yr, zs, zr,
):
    x, y, z, c = place()
    me = x * 2 + c
    greet(group_peers(x, y, z, c))

    def owner(k):
        return (z + zoff(NZ - 1 - k)) % NZ

    def xcopy(k, j):
        zi = owner(k)
        px, pc = slab_peer(x, c, j)
        return remote(
            p_ref.at[px * 2 + pc, zi], arrived.at[zi, pl.ds(2 * me, 2)], xs.at[k, j], xr.at[k, j],
            device(px, y, z, pc),
        )

    def local(k):
        zi = owner(k)
        return pltpu.make_async_copy(p_ref.at[me, zi], arrived.at[zi, pl.ds(2 * me, 2)], ls.at[k])

    def ycopy(k, d):
        return remote(
            ysend.at[k, d - 1], yrecv.at[k, d - 1], ys.at[k, d], yr.at[k, d],
            device(x, (y + d) % NY, z, c),
        )

    def zcopy(d):
        return remote(
            zsend.at[d - 1], zrecv.at[d - 1], zs.at[d], zr.at[d], device(x, y, (z + d) % NZ, c)
        )

    def push(k, carry):
        local(k).start()

        def each(j, carry):
            xcopy(k, j).start()
            return carry

        return lax.fori_loop(1, PEERS, each, carry)

    lax.fori_loop(0, NZ, push, 0)

    def merge(k):
        zi = owner(k)
        local(k).wait()

        def each(j, carry):
            sx, sc = slab_source(x, c, j)
            remote(
                p_ref.at[me, zi], arrived.at[zi, pl.ds(2 * (sx * 2 + sc), 2)],
                xs.at[k, j], xr.at[k, j], device(sx, y, z, sc),
            ).wait_recv()
            return carry

        lax.fori_loop(1, PEERS, each, 0)

        chunk[...] = arrived[zi]

        def run(i, total):
            at = zi * OWN + i
            total = total * keep[at] + chunk[order[at]].astype(F32)
            runs[i] = total
            return total

        lax.fori_loop(0, OWN, run, jnp.zeros((BLK, BLK), F32))
        for d in (1, 3, 2):
            base = zi * OWN + QTR * ((y + d) % NY)
            for b in range(QTR):
                ysend[k, d - 1, b] = (runs[last[base + b]] * has[base + b]).astype(BF16)
            ycopy(k, d).start()
        base = zi * OWN + QTR * y
        for b in range(QTR):
            yown[k, b] = runs[last[base + b]] * has[base + b]

    def total_of(k):
        for d in range(1, NY):
            ycopy(k, d).wait_recv()
        return [
            yown[k, b] + yrecv[k, 0, b].astype(F32) + yrecv[k, 1, b].astype(F32)
            + yrecv[k, 2, b].astype(F32)
            for b in range(QTR)
        ]

    def forward(k):
        d = zoff(NZ - 1 - k)
        for b, value in enumerate(total_of(k)):
            zsend[d - 1, b] = value.astype(BF16)
        zcopy(d).start()

    merge(0)

    def step(k, carry):
        merge(k)
        forward(k - 1)
        return carry

    lax.fori_loop(1, NZ, step, 0)
    for b, value in enumerate(total_of(NZ - 1)):
        o_ref[b] = value
    for d in (1, 7, 2, 6, 3, 5, 4):
        zcopy(d).wait_recv()
        for b in range(QTR):
            o_ref[b] += zrecv[d - 1, b].astype(F32)

    for d in range(1, NZ):
        zcopy(d).wait_send()

    def finish(k, carry):
        for d in range(1, NY):
            ycopy(k, d).wait_send()

        def each(j, carry):
            xcopy(k, j).wait_send()
            return carry

        return lax.fori_loop(1, PEERS, each, carry)

    lax.fori_loop(0, NZ, finish, 0)


def scatter_blocks(tables, partials):
    dma = pltpu.SemaphoreType.DMA
    smem = pl.BlockSpec(memory_space=pltpu.SMEM)
    return pl.pallas_call(
        scatter_kernel,
        name="scatter_blocks",
        out_shape=jax.ShapeDtypeStruct((QTR, BLK, BLK), F32),
        in_specs=[smem, smem, smem, smem, pl.BlockSpec(memory_space=pltpu.VMEM)],
        out_specs=pl.BlockSpec(memory_space=pltpu.VMEM),
        scratch_shapes=[
            pltpu.VMEM((NZ, OWN, BLK, BLK), BF16),
            pltpu.VMEM((OWN, BLK, BLK), BF16),
            pltpu.VMEM((OWN, BLK, BLK), F32),
            pltpu.VMEM((NZ, NY - 1, QTR, BLK, BLK), BF16),
            pltpu.VMEM((NZ, QTR, BLK, BLK), F32),
            pltpu.VMEM((NZ, NY - 1, QTR, BLK, BLK), BF16),
            pltpu.VMEM((NZ - 1, QTR, BLK, BLK), BF16),
            pltpu.VMEM((NZ - 1, QTR, BLK, BLK), BF16),
            dma((NZ,)),
            dma((NZ, PEERS)),
            dma((NZ, PEERS)),
            dma((NZ, NY)),
            dma((NZ, NY)),
            dma((NZ,)),
            dma((NZ,)),
        ],
        compiler_params=pltpu.CompilerParams(
            collective_id=1, has_side_effects=True, vmem_limit_bytes=VMEM_LIMIT
        ),
    )(*tables, partials)


GROUP = 8


def edge_kernel(forward, rounds, pick, put, adj_ref, rows_ref, o_ref, total):
    slots = rows_ref.shape[0]

    def clear(i, carry):
        total[i] = jnp.zeros((BLK, BLK), F32)
        return carry

    lax.fori_loop(0, slots, clear, 0)
    contract = (((1,), (0,)), ((), ())) if forward else (((0,), (0,)), ((), ()))

    def one_round(r, carry):
        terms = []
        for i in range(GROUP):
            k = r * GROUP + i
            terms.append(
                lax.dot_general(adj_ref[k], rows_ref[pick[k]], contract, preferred_element_type=F32)
            )
        for i in range(GROUP):
            at = put[r * GROUP + i]
            total[at] += terms[i]
        return carry

    lax.fori_loop(0, rounds[0], one_round, 0)

    def write(i, carry):
        o_ref[i] = total[i].astype(BF16)
        return carry

    lax.fori_loop(0, slots, write, 0)


def edge_terms(forward, rounds, pick, put, adj, rows):
    slots = rows.shape[0]
    smem = pl.BlockSpec(memory_space=pltpu.SMEM)
    vmem = pl.BlockSpec(memory_space=pltpu.VMEM)

    def run(*refs):
        edge_kernel(forward, *refs)

    return pl.pallas_call(
        run,
        name="edge_forward" if forward else "edge_backward",
        out_shape=jax.ShapeDtypeStruct(rows.shape, BF16),
        in_specs=[smem, smem, smem, vmem, vmem],
        out_specs=vmem,
        scratch_shapes=[pltpu.VMEM((slots + 1, BLK, BLK), F32)],
        compiler_params=pltpu.CompilerParams(vmem_limit_bytes=VMEM_LIMIT),
    )(rounds, pick, put, adj, rows)


SLAB = NX * NY * 2


def slab_device(x, y, z, c, j):
    return device((x + j // (2 * NY)) % NX, (y + (j // 2) % NY) % NY, z, (c + j) % 2)


def final_kernel(w_ref, a_ref, b_ref, oa_ref, ob_ref, ow_ref, first, mine, second, ls, gs, gr, s1, r1, s2, r2, s3, r3):
    x, y, z, c = place()
    me = (x * NY + y) * 2 + c
    rows = w_ref.shape[0] // SLAB
    height = a_ref.shape[0]

    def index(j):
        return (((x + j // (2 * NY)) % NX) * NY + (y + (j // 2) % NY) % NY) * 2 + (c + j) % 2

    def source(j):
        return (
            ((x + NX - j // (2 * NY)) % NX) * NY + (y + NY - (j // 2) % NY) % NY
        ) * 2 + (c + j) % 2

    peers = [slab_device(x, y, z, c, j) for j in range(1, SLAB)]
    peers += [device(x, y, (z + d) % NZ, c) for d in range(1, NZ)]
    greet(peers)

    def one(j):
        return remote(
            w_ref.at[pl.ds(rows * index(j), rows)], first.at[me], s1.at[j], r1.at[j],
            slab_device(x, y, z, c, j),
        )

    def two(d):
        return remote(mine.at[0], second.at[z], s2.at[d], r2.at[d], device(x, y, (z + d) % NZ, c))

    def three(j):
        return remote(
            mine.at[1], ow_ref.at[pl.ds(rows * me, rows)], s3.at[j], r3.at[j],
            slab_device(x, y, z, c, j),
        )

    def spread(i, d):
        src, dst = ((a_ref, oa_ref), (b_ref, ob_ref))[i]
        return remote(
            src, dst.at[pl.ds(height * y, height)], gs.at[i, d], gr.at[i, d],
            device(x, (y + d) % NY, z, c),
        )

    def loop(body):
        def run(j, carry):
            body(j)
            return carry

        lax.fori_loop(1, SLAB, run, 0)

    loop(lambda j: one(j).start())
    first[me] = w_ref[pl.ds(rows * me, rows)]
    locals_ = [
        pltpu.make_async_copy(src, dst.at[pl.ds(height * y, height)], ls.at[i])
        for i, (src, dst) in enumerate(((a_ref, oa_ref), (b_ref, ob_ref)))
    ]
    for i in (0, 1):
        locals_[i].start()
        for d in (1, 3, 2):
            spread(i, d).start()

    def arrived(j):
        remote(
            w_ref.at[pl.ds(0, rows)], first.at[source(j)], s1.at[j], r1.at[j], device(x, y, z, c)
        ).wait_recv()

    loop(arrived)
    mine[0] = jnp.sum(first[...], axis=0)
    for d in range(1, NZ):
        two(d).start()
    second[z] = mine[0]
    for d in range(1, NZ):
        remote(
            mine.at[0], second.at[(z + NZ - d) % NZ], s2.at[d], r2.at[d], device(x, y, z, c)
        ).wait_recv()
    mine[1] = jnp.sum(second[...], axis=0)
    loop(lambda j: three(j).start())
    ow_ref[pl.ds(rows * me, rows)] = mine[1]

    def landed(j):
        remote(
            mine.at[1], ow_ref.at[pl.ds(rows * source(j), rows)], s3.at[j], r3.at[j],
            device(x, y, z, c),
        ).wait_recv()

    loop(landed)
    loop(lambda j: one(j).wait_send())
    for d in range(1, NZ):
        two(d).wait_send()
    loop(lambda j: three(j).wait_send())
    for i in (0, 1):
        locals_[i].wait()
        for d in range(1, NY):
            spread(i, d).wait_send()
            src, dst = ((a_ref, oa_ref), (b_ref, ob_ref))[i]
            remote(
                src, dst.at[pl.ds(height * ((y + NY - d) % NY), height)], gs.at[i, d], gr.at[i, d],
                device(x, y, z, c),
            ).wait_recv()


def finish(weights, a, b):
    dma = pltpu.SemaphoreType.DMA
    vmem = pl.BlockSpec(memory_space=pltpu.VMEM)
    rows, height, hidden = weights.shape[0] // SLAB, a.shape[0], a.shape[1]
    return pl.pallas_call(
        final_kernel,
        name="finish",
        out_shape=(
            jax.ShapeDtypeStruct((NY * height, hidden), BF16),
            jax.ShapeDtypeStruct((NY * height, hidden), BF16),
            jax.ShapeDtypeStruct(weights.shape, F32),
        ),
        in_specs=[vmem, vmem, vmem],
        out_specs=(vmem, vmem, vmem),
        scratch_shapes=[
            pltpu.VMEM((SLAB, rows, hidden), F32),
            pltpu.VMEM((2, rows, hidden), F32),
            pltpu.VMEM((NZ, rows, hidden), F32),
            dma((2,)),
            dma((2, NY)),
            dma((2, NY)),
            dma((SLAB,)),
            dma((SLAB,)),
            dma((NZ,)),
            dma((NZ,)),
            dma((SLAB,)),
            dma((SLAB,)),
        ],
        compiler_params=pltpu.CompilerParams(
            collective_id=2, has_side_effects=True, vmem_limit_bytes=VMEM_LIMIT
        ),
    )(weights, a, b)


def slot_index(slot):
    x, z, c, s = slot // 32, (slot // 4) % NZ, (slot // 2) % 2, slot % 2
    return ((x * 2 + c) * NZ + z) * 2 + s


def run_tables(blocks):
    n = blocks.shape[1]
    at = jnp.arange(n, dtype=I32)
    mine, other = blocks[:, :, None], blocks[:, None, :]
    ahead = (other < mine) | ((other == mine) & (at[None, None, :] < at[None, :, None]))
    rank = jnp.sum(ahead.astype(I32), axis=2)
    hit = rank[:, :, None] == at[None, None, :]
    order = jnp.sum(jnp.where(hit, at[None, :, None], 0), axis=1)
    first = jnp.sum((other == mine) & (at[None, None, :] < at[None, :, None]), axis=2) == 0
    keep = jnp.sum(jnp.where(hit & ~first[:, :, None], 1.0, 0.0), axis=1)
    upto = jnp.sum((blocks[:, None, :] <= at[None, :, None]).astype(I32), axis=2)
    has = jnp.any(blocks[:, None, :] == at[None, :, None], axis=2)
    return (
        order.reshape(-1),
        keep.astype(F32).reshape(-1),
        jnp.maximum(upto - 1, 0).reshape(-1),
        has.astype(F32).reshape(-1),
    )


def relay_tables(send_src, recv_dst):
    both = jnp.concatenate([send_src.reshape(NX, NZ, 2, 2), recv_dst.reshape(NX, NZ, 2, 2)], axis=3)
    both = both.transpose(1, 0, 2, 3).reshape(NZ, PEERS * 4)
    groups = [[(x * NZ + z) * 2 + c for z in range(NZ)] for x in range(NX) for c in range(2)]
    both = lax.all_to_all(
        both, "edge", split_axis=0, concat_axis=0, axis_index_groups=groups, tiled=True
    ).reshape(NZ, PEERS, 4)
    return both[:, :, :2].reshape(NZ, OWN), both[:, :, 2:].reshape(NZ, OWN)


def body(
    node_feat, cotangent, w_msg, w_self, adjacency, edge_src, edge_dst, send_src, recv_dst, live
):
    hidden = node_feat.shape[1]
    quarter = node_feat.shape[0] // NY
    plane = lax.axis_index("feat")
    nodes = lax.dynamic_slice_in_dim(node_feat, plane * quarter, quarter, 0)
    cot = lax.dynamic_slice_in_dim(cotangent, plane * quarter, quarter, 0)

    src_blocks, dst_blocks = relay_tables(send_src, recv_dst)
    adj = adjacency.reshape(-1, BLK, BLK)
    edges = adj.shape[0]
    alive = jnp.arange(edges, dtype=I32) < live.reshape(())
    rounds = ((live.reshape(1) + GROUP - 1) // GROUP).astype(I32)
    src_slot = slot_index(edge_src.reshape(-1))
    dst_slot = slot_index(edge_dst.reshape(-1))
    slots = PEERS * NZ * 2

    def gather(blocks, rows):
        got = gather_blocks(blocks.reshape(-1), rows.reshape(QTR, BLK, hidden))
        return got.reshape(slots, BLK, hidden)

    def scatter(blocks, parts):
        total = scatter_blocks(run_tables(blocks), parts.reshape(PEERS, NZ, 2, BLK, hidden))
        return total.reshape(quarter, hidden)

    messages = jnp.dot(nodes, w_msg, preferred_element_type=F32).astype(BF16)
    incoming = gather(src_blocks, messages)
    parts = edge_terms(True, rounds, src_slot, jnp.where(alive, dst_slot, slots), adj, incoming)
    aggregate = scatter(dst_blocks, parts)
    preact = jnp.dot(nodes, w_self, preferred_element_type=F32) + aggregate
    sig = jax.nn.sigmoid(preact)
    out = (preact * sig).astype(BF16)
    grad_pre = (cot.astype(F32) * sig * (1.0 + preact * (1.0 - sig))).astype(BF16)
    rows_of = (((0,), (0,)), ((), ()))
    wself = lax.dot_general(nodes, grad_pre, rows_of, preferred_element_type=F32)
    grad_in = gather(dst_blocks, grad_pre)
    grad_parts = edge_terms(False, rounds, dst_slot, jnp.where(alive, src_slot, slots), adj, grad_in)
    grad_msg = scatter(src_blocks, grad_parts).astype(BF16)
    wmsg = lax.dot_general(nodes, grad_msg, rows_of, preferred_element_type=F32)
    grad_feat = (
        jnp.dot(grad_pre, w_self.T, preferred_element_type=F32)
        + jnp.dot(grad_msg, w_msg.T, preferred_element_type=F32)
    ).astype(BF16)
    out, grad_feat, weights = finish(jnp.concatenate([wmsg, wself], axis=0), out, grad_feat)
    return out, grad_feat, weights[:hidden], weights[hidden:]


def solution(mesh):
    in_specs = (
        P("edge", None),
        P("edge", None),
        P(),
        P(),
        P("edge", "feat", None, None, None),
        P("edge", "feat", None),
        P("edge", "feat", None),
        P("edge", "feat", None, None),
        P("edge", "feat", None, None),
        P("edge", "feat"),
    )
    out_specs = (P("edge", None), P("edge", None), P(), P())
    return jax.shard_map(body, mesh=mesh, in_specs=in_specs, out_specs=out_specs, check_vma=False)
```

time: 927 us -> 339 us (0.37)
  waiting for transfers between devices: 685 us -> 2.97 us
  Pallas kernels: 0 us -> 301 us
  other arithmetic: 63.8 us -> 4.59 us
  blocking collectives: 52.7 us -> 0 us
  starting transfers between devices: 61.6 us -> 9 us
  local copies, waits for them, and re-layouts: 37.4 us -> 14.5 us
  between operations: 15 us -> 1.48 us
    all_to_all x5 -> x1, waiting for transfers between devices: 620 us -> 2.97 us  [relay_tables(): lax.all_to_all(both, 'edge', split_axis=0, concat_axis=0, axis_index_grou...]
    pallas_call x0 -> x7, Pallas kernels: none -> 301 us  [the longest x2 132 us: gather_blocks(): pl.pallas_call(gather_kernel, name='gather_blocks', out_shape=jax.ShapeDt...]
    all_gather x2 -> x0, waiting for transfers between devices: 65.1 us -> none  [over_pieces(): return lax.all_gather(value, axis).sum(0)]
    all_to_all x1 -> x0, blocking collectives: 52.7 us -> none  [sent_to_all(): lax.all_to_all(jnp.broadcast_to(value[None], (peers, *value.shape)), axis...]
    all_to_all x5 -> x1, starting transfers between devices: 61.5 us -> 9 us  [relay_tables(): lax.all_to_all(both, 'edge', split_axis=0, concat_axis=0, axis_index_grou...]
    scatter-add x4 -> x0, other arithmetic: 46.5 us -> none  [the longest x1 17 us: body(): grad_owner = jnp.zeros((owned_blocks, block_size, hidden), jnp.float32).a...]
    gather x4 -> x0, local copies, waits for them, and re-layouts: 13.8 us -> none  [the longest x2 7.69 us: one_round(): jnp.take(source_rows, picks, axis=0)]
  transfers between devices with their start and end apart: 7 -> 1, of which waited for: 6 -> 1; matrix products, arithmetic and copies ran while one was open for 3% -> 1% of each run, Pallas kernels for 0% -> 0%
where the time goes in v1:
time: 339 us; the launch traced here: 338 us
  Pallas kernels  301 us (89%)
  local copies, waits for them, and re-layouts  14.5 us (4%)
  starting transfers between devices  9 us (3%)
  matrix products  5.02 us (1%)
  other arithmetic  4.59 us (1%)
    pallas_call x2, Pallas kernels, gather_blocks(): pl.pallas_call(gather_kernel, name='gather_blocks', out_shape=jax.ShapeDt...  132 us
    pallas_call x2, Pallas kernels, scatter_blocks(): pl.pallas_call(scatter_kernel, name='scatter_blocks', out_shape=jax.Shape...  126 us
    pallas_call x1, Pallas kernels, finish(): pl.pallas_call(final_kernel, name='finish', out_shape=(jax.ShapeDtypeStru...  24.9 us
    pallas_call x2, Pallas kernels, edge_terms(): pl.pallas_call(run, name='edge_forward' if forward else 'edge_backward',...  17.1 us
    all_to_all x1, starting transfers between devices, relay_tables(): lax.all_to_all(both, 'edge', split_axis=0, concat_axis=0, axis_index_grou...  9 us
  transfers between devices with their start and end apart: 1, of which 1 were waited for; matrix products, arithmetic and copies ran while one was open for 1% of the time, Pallas kernels for 0%

profile of v1, /device:TPU:1, one launch (start us, length us, event | category | flops | bytes accessed | tf_op | source)
XLA Modules:
  0.0 338.1 jit_solution(4187824364353574819)
XLA Ops:
  0.6 0.8 reshape.127
  1.6 0.8 reshape.128
  2.5 0.7 copy.39
  3.2 9.0 %all-to-all-start = ((s32[8,1,32]{2,1,0:T(1,128)}), s32[8,1,32]{2,1,0:T(1,128)S(1)}, u32[]{:S(2)}, u32[]{:S(2)}) async-start(s32[8,1,32]{2,1,0:T(1,128)} %copy.39), calls=%async_computation | async-start | bytes 8192 | tf_op jit(solution)/shard_map/all_to_all | solution.py:569
  12.9 1.6 convolution_convert_fusion
  14.5 1.2 compare_select_fusion.8
  15.7 3.0 all-to-all-done
  18.9 0.7 reshape_reshape.7.tab
  20.3 1.0 convert_reduce_fusion.1
  24.0 67.2 %gather_blocks.2 = bf16[8,8,2,128,128]{4,3,2,1,0:T(8,128)(2,1)} custom-call(s32[128]{0:T(128)} %reshape_reshape.7.tab, bf16[4,128,128]{2,1,0:T(8,128)(2,1)} %bitcast.77), custom_call_target="tpu_custom_call" | custom-call | tf_op jit(solution)/shard_map/gather_blocks/pallas_call | solution.py:166
  91.2 8.4 %edge_forward.1 = bf16[128,128,128]{2,1,0:T(8,128)(2,1)} custom-call(s32[1]{0:T(128)S(6)} %select_n.80.refs_0_, s32[64]{0:T(128)} %get-tuple-element.30.refs_1_, s32[64]{0:T(128)} %get-tuple-element.21.refs_2_, bf16[64,128,128]{2,1,0:T(8,128)(2,1)} %bitcast.72, bf16[128,128,128]{2,1,0:T(8,128)(2,1)} %bitcast.71), custom_call_target="tpu_custom_call" | custom-call | tf_op jit(solution)/shard_map/edge_forward/pallas_call | solution.py:390
  99.6 63.2 %scatter_blocks.2 = f32[4,128,128]{2,1,0:T(8,128)} custom-call(s32[128]{0:T(128)} %reshape.136.order, f32[128]{0:T(128)} %reshape.137.keep, s32[128]{0:T(128)} %max.17.last, f32[128]{0:T(128)} %reshape.146.has, bf16[8,8,2,128,128]{4,3,2,1,0:T(8,128)(2,1)} %bitcast.69), custom_call_target="tpu_custom_call" | custom-call | tf_op jit(solution)/shard_map/scatter_blocks/pallas_call | solution.py:319
  162.8 2.0 multiply_convert_fusion
  165.1 0.7 reshape_reshape.6.tab
  168.3 65.0 %gather_blocks.3 = bf16[8,8,2,128,128]{4,3,2,1,0:T(8,128)(2,1)} custom-call(s32[128]{0:T(128)} %reshape_reshape.6.tab, bf16[4,128,128]{2,1,0:T(8,128)(2,1)} %bitcast.76), custom_call_target="tpu_custom_call" | custom-call | tf_op jit(solution)/shard_map/gather_blocks/pallas_call | solution.py:166
  233.3 8.7 %edge_backward.1 = bf16[128,128,128]{2,1,0:T(8,128)(2,1)} custom-call(s32[1]{0:T(128)S(6)} %select_n.80.refs_0_, s32[64]{0:T(128)} %get-tuple-element.22.refs_1_, s32[64]{0:T(128)} %get-tuple-element.29.refs_2_, bf16[64,128,128]{2,1,0:T(8,128)(2,1)} %bitcast.73, bf16[128,128,128]{2,1,0:T(8,128)(2,1)} %bitcast.70), custom_call_target="tpu_custom_call" | custom-call | tf_op jit(solution)/shard_map/edge_backward/pallas_call | solution.py:390
  242.0 63.2 %scatter_blocks.3 = f32[4,128,128]{2,1,0:T(8,128)} custom-call(s32[128]{0:T(128)} %reshape.130.order, f32[128]{0:T(128)} %reshape.131.keep, s32[128]{0:T(128)} %max.15.last, f32[128]{0:T(128)} %reshape.145.has, bf16[8,8,2,128,128]{4,3,2,1,0:T(8,128)(2,1)} %bitcast.68), custom_call_target="tpu_custom_call" | custom-call | tf_op jit(solution)/shard_map/scatter_blocks/pallas_call | solution.py:319
  305.2 1.0 convert_element_type.66
  306.4 0.8 fusion.b_ref
  307.2 0.7 pad_maximum_fusion.w_ref
  307.9 24.9 %finish.1 = (bf16[2048,128]{1,0:T(8,128)(2,1)}, bf16[2048,128]{1,0:T(8,128)(2,1)}, f32[256,128]{1,0:T(8,128)}) custom-call(f32[256,128]{1,0:T(8,128)} %pad_maximum_fusion.w_ref, bf16[512,128]{1,0:T(8,128)(2,1)} %get-tuple-element.23.a_ref, bf16[512,128]{1,0:T(8,128)(2,1)} %fusion.b_ref), custom_call_target="tpu_custom_call" | custom-call | tf_op jit(solution)/shard_map/finish/pallas_call | solution.py:510
  332.8 1.5 fusion.29
  334.3 1.9 copy.50
  336.2 1.9 copy.51
  (38 shorter events, 6.8 us)
Async XLA Ops:
  0.6 12.2 %copy-start = (bf16[2048,128]{1,0:T(8,128)(2,1)S(1)}, bf16[2048,128]{1,0:T(8,128)(2,1)}, u32[]{:S(2)}) copy-start(bf16[2048,128]{1,0:T(8,128)(2,1)} %param.10) | copy-start | bytes 1572868
  3.2 15.5 %all-to-all-start = ((s32[8,1,32]{2,1,0:T(1,128)}), s32[8,1,32]{2,1,0:T(1,128)S(1)}, u32[]{:S(2)}, u32[]{:S(2)}) async-start(s32[8,1,32]{2,1,0:T(1,128)} %copy.39), calls=%async_computation | async-start | bytes 8192 | tf_op jit(solution)/shard_map/all_to_all | solution.py:569
  99.6 63.2 %copy-start.3 = (bf16[128,128]{1,0:T(8,128)(2,1)S(1)}, bf16[128,128]{1,0:T(8,128)(2,1)}, u32[]{:S(2)}) copy-start(bf16[128,128]{1,0:T(8,128)(2,1)} %param.13) | copy-start | bytes 98308
  164.7 3.5 %copy-start.1 = (bf16[512,128]{1,0:T(8,128)(2,1)}, bf16[512,128]{1,0:T(8,128)(2,1)S(1)}, u32[]{:S(2)}) copy-start(bf16[512,128]{1,0:T(8,128)(2,1)S(1)} %get-tuple-element.24) | copy-start | bytes 393220
  242.0 64.4 %copy-start.2 = (bf16[128,128]{1,0:T(8,128)(2,1)S(1)}, bf16[128,128]{1,0:T(8,128)(2,1)}, u32[]{:S(2)}) copy-start(bf16[128,128]{1,0:T(8,128)(2,1)} %param.12) | copy-start | bytes 98308

commit v2 on v0

v2 whole, which is shorter than its diff:
```python
import jax
import jax.numpy as jnp
from jax import lax
from jax.experimental import pallas as pl
from jax.experimental.pallas import tpu as pltpu
from jax.sharding import PartitionSpec as P

MESH = pl.DeviceIdType.MESH
NX, NY, NZ = 4, 4, 8
BLK = 128
OWN = 16
QTR = OWN // NY
PEERS = 2 * NX
VMEM_LIMIT = 60 * 1024 * 1024
GROUP = 8
SLAB = NX * NY * 2
CHUNK = 2 * PEERS
EDGES = 64
SLOTS = 128
SRC, SRC_PREV, SRC_LAST, DST, DST_PREV, DST_LAST = range(6)
BF16, F32, I32 = jnp.bfloat16, jnp.float32, jnp.int32


def place():
    edge = lax.axis_index("edge")
    y = lax.axis_index("feat")
    return edge // 16, y, (edge // 2) % NZ, edge % 2


def device(x, y, z, c):
    return ((x * NZ + z) * 2 + c, y)


def zoff(k):
    return ((2 * (k % 2) - 1) * ((k + 1) // 2) + NZ) % NZ


def remote(src, dst, send, recv, peer):
    return pltpu.make_async_remote_copy(
        src_ref=src, dst_ref=dst, send_sem=send, recv_sem=recv, device_id=peer, device_id_type=MESH
    )


def slab_peer(x, c, j):
    return (x + j // 2) % NX, (c + j) % 2


def slab_source(x, c, j):
    return (x + NX - j // 2) % NX, (c + j) % 2


def slab_device(x, y, z, c, j):
    return device((x + j // (2 * NY)) % NX, (y + (j // 2) % NY) % NY, z, (c + j) % 2)


def loop(first, stop, body):
    def run(i, carry):
        body(i)
        return carry

    lax.fori_loop(first, stop, run, 0)


def dot(a, b, contract):
    return lax.dot_general(a, b, (contract, ((), ())), preferred_element_type=F32)


def tables_kernel(blocks_ref, edges_ref, meta_ref, etab_ref):
    shape = blocks_ref.shape
    blocks = blocks_ref[...]
    lane = lax.broadcasted_iota(I32, shape, 1)
    prev = jnp.full(shape, CHUNK, I32)
    for d in range(CHUNK - 1, 0, -1):
        same = (pltpu.roll(blocks, d, 1) == blocks) & (lane >= d) & (lane < CHUNK)
        prev = jnp.where(same, lane - d, prev)
    last = jnp.full(shape, CHUNK, I32)
    for i in range(CHUNK):
        last = jnp.where(blocks[:, i : i + 1] == lane, i, last)
    for row, (value, at) in enumerate(
        ((blocks, 0), (prev, 0), (last, 0), (blocks, NZ), (prev, NZ), (last, NZ))
    ):
        for z in range(NZ):
            meta_ref[z, row : row + 1] = value[at + z : at + z + 1]

    wide = (SLOTS, SLOTS)
    down = lax.broadcasted_iota(I32, wide, 0)
    along = lax.broadcasted_iota(I32, wide, 1)
    downf, alongf = down.astype(F32), along.astype(F32)
    live = edges_ref[2:3, :]
    none = float(EDGES)
    for row, prev_row, last_row in ((0, SRC_PREV, SRC_LAST), (1, DST_PREV, DST_LAST)):
        slot = edges_ref[row : row + 1, :]
        etab_ref[(SRC, DST)[row] : (SRC, DST)[row] + 1] = slot
        on = lax.broadcasted_iota(I32, slot.shape, 1) < live
        flat = jnp.where(on, slot.astype(F32), -1.0)
        tall = jnp.sum(jnp.where(down == along, flat, 0.0), axis=1, keepdims=True)
        before = jnp.where((tall == flat) & (down < along) & (tall >= 0.0), downf, -1.0)
        found = jnp.max(before, axis=0, keepdims=True)
        etab_ref[prev_row : prev_row + 1] = jnp.where(found < 0.0, none, found).astype(I32)
        ends = jnp.max(jnp.where(tall == alongf, downf, -1.0), axis=0, keepdims=True)
        etab_ref[last_row : last_row + 1] = jnp.where(ends < 0.0, none, ends).astype(I32)


def tables(blocks, edges):
    return pl.pallas_call(
        tables_kernel,
        name="tables",
        out_shape=(
            jax.ShapeDtypeStruct((NZ, 8, SLOTS), I32),
            jax.ShapeDtypeStruct((8, SLOTS), I32),
        ),
    )(blocks, edges)


def layer_kernel(
    etab, meta_ref, nf_ref, cot_ref, wm_ref, ws_ref, adj_ref,
    out_ref, gf_ref, ow_ref,
    meta_in, meta, adj, dense, chunk, staged, rows, chain, parts, arrived, runs,
    ysend, yown, yrecv, zsend, zrecv, total, pre, weights, first, mine, second,
    al, ml, ms, mr, g_zs, g_zr, g_ys, g_yr, g_xs, g_xr,
    ls, s_xs, s_xr, s_ys, s_yr, s_zs, s_zr, gs, gr, s1, r1, s2, r2, s3, r3,
):
    x, y, z, c = place()
    me = x * 2 + c
    quarter = QTR * BLK
    here = device(x, y, z, c)
    mine_rows = pl.ds(quarter * y, quarter)
    own = pl.ds(QTR * y, QTR)

    barrier = pltpu.get_barrier_semaphore()
    peers = [slab_device(x, y, z, c, j) for j in range(1, SLAB)]
    peers += [device(x, y, (z + d) % NZ, c) for d in range(1, NZ)]
    for peer in peers:
        pl.semaphore_signal(barrier, inc=1, device_id=peer, device_id_type=MESH)

    adj_copy = pltpu.make_async_copy(adj_ref, adj, al)
    adj_copy.start()
    own_meta = pltpu.make_async_copy(meta_ref.at[z], meta.at[z], ml.at[0])
    own_meta.start()

    def project(i):
        b = (QTR * y + i) % OWN
        node = nf_ref[pl.ds(pl.multiple_of(b * BLK, BLK), BLK)]
        dense[z, b] = dot(node, wm_ref[...], ((1,), (0,))).astype(BF16)

    loop(0, OWN, project)
    pl.semaphore_wait(barrier, len(peers))

    def slots_of(px, zi, pc):
        return pl.ds(((px * NZ + zi) * 2 + pc) * 2, 2)

    def gather(forward):
        block_row = SRC if forward else DST

        def mcopy(d):
            return remote(
                meta_ref.at[(z + d) % NZ], meta_in.at[z], ms.at[d], mr.at[d],
                device(x, y, (z + d) % NZ, c),
            )

        def zcopy(d):
            part = dense.at[z, own]
            return remote(part, part, g_zs.at[d], g_zr.at[d], device(x, y, (z + d) % NZ, c))

        def ycopy(k, zi, d):
            part = dense.at[zi, own]
            return remote(part, part, g_ys.at[k, d], g_yr.at[k, d], device(x, (y + d) % NY, z, c))

        def xcopy(k, zi, j):
            px, pc = slab_peer(x, c, j)
            return remote(
                staged.at[px * 2 + pc, zi], rows.at[slots_of(x, zi, c)], g_xs.at[k, j], g_xr.at[k, j],
                device(px, y, z, pc),
            )

        def meta_load(k, zi):
            return pltpu.make_async_copy(meta_in.at[zi], meta.at[zi], ml.at[k])

        def spread(k):
            d = zoff(k)
            zi = (z + NZ - d) % NZ
            part = dense.at[zi, own]
            if forward:
                remote(meta_ref.at[z], meta_in.at[zi], ms.at[d], mr.at[d], here).wait_recv()
                meta_load(k, zi).start()
            remote(part, part, g_zs.at[d], g_zr.at[d], here).wait_recv()
            for dy in (1, 3, 2):
                ycopy(k, zi, dy).start()

        def collect(k):
            zi = (z + NZ - zoff(k)) % NZ
            for dy in (1, 3, 2):
                part = dense.at[zi, pl.ds(QTR * ((y + NY - dy) % NY), QTR)]
                remote(part, part, g_ys.at[k, dy], g_yr.at[k, dy], here).wait_recv()
            if forward:
                meta_load(k, zi).wait()

        def deliver(k):
            zi = (z + NZ - zoff(k)) % NZ
            chunk[...] = dense[zi]

            def pick(j):
                px, pc = slab_peer(x, c, j)
                pid = px * 2 + pc
                for s in range(2):
                    staged[pid, zi, s] = chunk[meta[zi, block_row, pid * 2 + s]]

            loop(1, PEERS, pick)
            base = ((x * NZ + zi) * 2 + c) * 2
            for s in range(2):
                rows[base + s] = chunk[meta[zi, block_row, me * 2 + s]]
            loop(1, PEERS, lambda j: xcopy(k, zi, j).start())

        for d in (1, 7, 2, 6, 3, 5, 4):
            if forward:
                mcopy(d).start()
            zcopy(d).start()
        if forward:
            own_meta.wait()
            deliver(0)
            spread(1)
        else:
            for dy in (1, 3, 2):
                ycopy(0, z, dy).start()
            spread(1)
            collect(0)
            deliver(0)

        def step(k):
            @pl.when(k < NZ - 1)
            def _():
                spread(k + 1)

            collect(k)
            deliver(k)

        loop(1, NZ, step)

        for d in range(1, NZ):
            if forward:
                mcopy(d).wait_send()
            zcopy(d).wait_send()

        def finish(k):
            zi = (z + NZ - zoff(k)) % NZ

            def each(j):
                xcopy(k, zi, j).wait_send()
                sx, sc = slab_source(x, c, j)
                remote(
                    staged.at[me, zi], rows.at[slots_of(sx, zi, sc)], g_xs.at[k, j], g_xr.at[k, j], here
                ).wait_recv()

            loop(1, PEERS, each)

        loop(0, NZ, finish)

        def sent(k):
            zi = (z + NZ - zoff(k)) % NZ
            for dy in range(1, NY):
                ycopy(k, zi, dy).wait_send()

        loop(1 if forward else 0, NZ, sent)

    def edges(forward):
        pick, prev = (SRC, DST_PREV) if forward else (DST, SRC_PREV)
        contract = ((1,), (0,)) if forward else ((0,), (0,))
        chain[EDGES] = jnp.zeros((BLK, BLK), F32)

        def one_round(r):
            terms = []
            for i in range(GROUP):
                k = r * GROUP + i
                terms.append(dot(adj[k], rows[etab[pick, k]], contract))
            for i in range(GROUP):
                k = r * GROUP + i
                chain[k] = terms[i] + chain[etab[prev, k]]

        loop(0, EDGES // GROUP, one_round)

    def scatter(forward):
        end = DST_LAST if forward else SRC_LAST
        run_prev, run_last = (DST_PREV, DST_LAST) if forward else (SRC_PREV, SRC_LAST)

        def owner(k):
            return (z + zoff(NZ - 1 - k)) % NZ

        def xcopy(k, j):
            zi = owner(k)
            px, pc = slab_peer(x, c, j)
            return remote(
                parts.at[slots_of(px, zi, pc)], arrived.at[zi, pl.ds(2 * me, 2)],
                s_xs.at[k, j], s_xr.at[k, j], device(px, y, z, pc),
            )

        def local(k):
            zi = owner(k)
            return pltpu.make_async_copy(
                parts.at[slots_of(x, zi, c)], arrived.at[zi, pl.ds(2 * me, 2)], ls.at[k]
            )

        def ycopy(k, d):
            return remote(
                ysend.at[k, d - 1], yrecv.at[k, d - 1], s_ys.at[k, d], s_yr.at[k, d],
                device(x, (y + d) % NY, z, c),
            )

        def zcopy(d):
            return remote(
                zsend.at[d - 1], zrecv.at[d - 1], s_zs.at[d], s_zr.at[d], device(x, y, (z + d) % NZ, c)
            )

        def write(k):
            zi = owner(k)

            def each(pid):
                base = (((pid // 2) * NZ + zi) * 2 + pid % 2) * 2
                for s in range(2):
                    parts[base + s] = chain[etab[end, base + s]].astype(BF16)

            loop(0, PEERS, each)

        def push(k):
            local(k).start()
            loop(1, PEERS, lambda j: xcopy(k, j).start())

        write(0)

        def issue(k):
            write(k)
            push(k - 1)

        loop(1, NZ, issue)
        push(NZ - 1)

        runs[CHUNK] = jnp.zeros((BLK, BLK), F32)

        def merge(k):
            zi = owner(k)
            local(k).wait()

            def each(j):
                sx, sc = slab_source(x, c, j)
                remote(
                    parts.at[slots_of(x, zi, c)], arrived.at[zi, pl.ds(2 * (sx * 2 + sc), 2)],
                    s_xs.at[k, j], s_xr.at[k, j], here,
                ).wait_recv()

            loop(1, PEERS, each)

            def run(i):
                runs[i] = arrived[zi, i].astype(F32) + runs[meta[zi, run_prev, i]]

            loop(0, CHUNK, run)
            for d in (1, 3, 2):
                base = QTR * ((y + d) % NY)
                for b in range(QTR):
                    ysend[k, d - 1, b] = runs[meta[zi, run_last, base + b]].astype(BF16)
                ycopy(k, d).start()
            for b in range(QTR):
                yown[k, b] = runs[meta[zi, run_last, QTR * y + b]]

        def total_of(k):
            for d in range(1, NY):
                ycopy(k, d).wait_recv()
            return [
                yown[k, b] + yrecv[k, 0, b].astype(F32) + yrecv[k, 1, b].astype(F32)
                + yrecv[k, 2, b].astype(F32)
                for b in range(QTR)
            ]

        def pass_on(k):
            d = zoff(NZ - 1 - k)
            for b, value in enumerate(total_of(k)):
                zsend[d - 1, b] = value.astype(BF16)
            zcopy(d).start()

        merge(0)

        def step(k):
            merge(k)
            pass_on(k - 1)

        loop(1, NZ, step)
        for b, value in enumerate(total_of(NZ - 1)):
            total[b] = value
        for d in (1, 7, 2, 6, 3, 5, 4):
            zcopy(d).wait_recv()
            for b in range(QTR):
                total[b] += zrecv[d - 1, b].astype(F32)

        for d in range(1, NZ):
            zcopy(d).wait_send()

        def finish(k):
            for d in range(1, NY):
                ycopy(k, d).wait_send()
            loop(1, PEERS, lambda j: xcopy(k, j).wait_send())

        loop(0, NZ, finish)

    def share(i, d):
        part = (out_ref, gf_ref)[i].at[mine_rows]
        return remote(part, part, gs.at[i, d], gr.at[i, d], device(x, (y + d) % NY, z, c))

    def shared(i):
        for d in range(1, NY):
            share(i, d).wait_send()
            part = (out_ref, gf_ref)[i].at[pl.ds(quarter * ((y + NY - d) % NY), quarter)]
            remote(part, part, gs.at[i, d], gr.at[i, d], here).wait_recv()

    def block_rows(b):
        return pl.ds(pl.multiple_of((QTR * y + b) * BLK, BLK), BLK)

    gather(True)
    adj_copy.wait()
    edges(True)
    scatter(True)

    def activate(b):
        node = nf_ref[block_rows(b)]
        preact = dot(node, ws_ref[...], ((1,), (0,))) + total[b]
        sig = jax.nn.sigmoid(preact)
        out_ref[block_rows(b)] = (preact * sig).astype(BF16)
        grad = cot_ref[block_rows(b)].astype(F32) * sig * (1.0 + preact * (1.0 - sig))
        grad = grad.astype(BF16)
        pre[b] = grad
        dense[z, QTR * y + b] = grad

    def outer(at, b, value):
        term = dot(nf_ref[block_rows(b)], value, ((0,), (0,)))
        if b == 0:
            weights[at : at + BLK] = term
        else:
            weights[at : at + BLK] += term

    for b in range(QTR):
        activate(b)
    for b in range(QTR):
        outer(BLK, b, pre[b])

    gather(False)
    edges(False)
    for d in (1, 3, 2):
        share(0, d).start()
    scatter(False)

    for b in range(QTR):
        outer(0, b, total[b].astype(BF16))

    height = 2 * BLK // SLAB
    slab_me = (x * NY + y) * 2 + c

    def index(j):
        return (((x + j // (2 * NY)) % NX) * NY + (y + (j // 2) % NY) % NY) * 2 + (c + j) % 2

    def source(j):
        return (
            ((x + NX - j // (2 * NY)) % NX) * NY + (y + NY - (j // 2) % NY) % NY
        ) * 2 + (c + j) % 2

    def one(j):
        return remote(
            weights.at[pl.ds(height * index(j), height)], first.at[slab_me], s1.at[j], r1.at[j],
            slab_device(x, y, z, c, j),
        )

    def two(d):
        return remote(mine.at[0], second.at[z], s2.at[d], r2.at[d], device(x, y, (z + d) % NZ, c))

    def three(j):
        return remote(
            mine.at[1], ow_ref.at[pl.ds(height * slab_me, height)], s3.at[j], r3.at[j],
            slab_device(x, y, z, c, j),
        )

    loop(1, SLAB, lambda j: one(j).start())
    first[slab_me] = weights[pl.ds(height * slab_me, height)]
    for b in range(QTR):
        gf_ref[block_rows(b)] = (
            dot(pre[b], ws_ref[...], ((1,), (1,)))
            + dot(total[b].astype(BF16), wm_ref[...], ((1,), (1,)))
        ).astype(BF16)
    for d in (1, 3, 2):
        share(1, d).start()
    loop(
        1, SLAB,
        lambda j: remote(
            weights.at[pl.ds(0, height)], first.at[source(j)], s1.at[j], r1.at[j], here
        ).wait_recv(),
    )
    mine[0] = jnp.sum(first[...], axis=0)
    for d in range(1, NZ):
        two(d).start()
    second[z] = mine[0]
    for d in range(1, NZ):
        remote(mine.at[0], second.at[(z + NZ - d) % NZ], s2.at[d], r2.at[d], here).wait_recv()
    mine[1] = jnp.sum(second[...], axis=0)
    loop(1, SLAB, lambda j: three(j).start())
    ow_ref[pl.ds(height * slab_me, height)] = mine[1]
    loop(
        1, SLAB,
        lambda j: remote(
            mine.at[1], ow_ref.at[pl.ds(height * source(j), height)], s3.at[j], r3.at[j], here
        ).wait_recv(),
    )
    loop(1, SLAB, lambda j: one(j).wait_send())
    for d in range(1, NZ):
        two(d).wait_send()
    loop(1, SLAB, lambda j: three(j).wait_send())
    shared(0)
    shared(1)


def layer(etab, meta, nf, cot, wm, ws, adj):
    dma = pltpu.SemaphoreType.DMA
    vmem = pl.BlockSpec(memory_space=pltpu.VMEM)
    hidden = nf.shape[1]
    block = (BLK, hidden)
    height = 2 * BLK // SLAB
    return pl.pallas_call(
        layer_kernel,
        name="layer",
        out_shape=(
            jax.ShapeDtypeStruct(nf.shape, BF16),
            jax.ShapeDtypeStruct(nf.shape, BF16),
            jax.ShapeDtypeStruct((2 * hidden, hidden), F32),
        ),
        in_specs=[pl.BlockSpec(memory_space=pltpu.SMEM), vmem, vmem, vmem, vmem, vmem, pl.BlockSpec(memory_space=pl.ANY)],
        out_specs=(vmem, vmem, vmem),
        scratch_shapes=[
            pltpu.VMEM((NZ, 8, SLOTS), I32),
            pltpu.SMEM((NZ, 8, SLOTS), I32),
            pltpu.VMEM((EDGES, BLK, BLK), BF16),
            pltpu.VMEM((NZ, OWN, *block), BF16),
            pltpu.VMEM((OWN, *block), BF16),
            pltpu.VMEM((PEERS, NZ, 2, *block), BF16),
            pltpu.VMEM((SLOTS, *block), BF16),
            pltpu.VMEM((EDGES + 1, *block), F32),
            pltpu.VMEM((SLOTS, *block), BF16),
            pltpu.VMEM((NZ, CHUNK, *block), BF16),
            pltpu.VMEM((CHUNK + 1, *block), F32),
            pltpu.VMEM((NZ, NY - 1, QTR, *block), BF16),
            pltpu.VMEM((NZ, QTR, *block), F32),
            pltpu.VMEM((NZ, NY - 1, QTR, *block), BF16),
            pltpu.VMEM((NZ - 1, QTR, *block), BF16),
            pltpu.VMEM((NZ - 1, QTR, *block), BF16),
            pltpu.VMEM((QTR, *block), F32),
            pltpu.VMEM((QTR, *block), BF16),
            pltpu.VMEM((2 * hidden, hidden), F32),
            pltpu.VMEM((SLAB, height, hidden), F32),
            pltpu.VMEM((2, height, hidden), F32),
            pltpu.VMEM((NZ, height, hidden), F32),
            dma,
            dma((NZ,)),
            dma((NZ,)),
            dma((NZ,)),
            dma((NZ,)),
            dma((NZ,)),
            dma((NZ, NY)),
            dma((NZ, NY)),
            dma((NZ, PEERS)),
            dma((NZ, PEERS)),
            dma((NZ,)),
            dma((NZ, PEERS)),
            dma((NZ, PEERS)),
            dma((NZ, NY)),
            dma((NZ, NY)),
            dma((NZ,)),
            dma((NZ,)),
            dma((2, NY)),
            dma((2, NY)),
            dma((SLAB,)),
            dma((SLAB,)),
            dma((NZ,)),
            dma((NZ,)),
            dma((SLAB,)),
            dma((SLAB,)),
        ],
        compiler_params=pltpu.CompilerParams(
            collective_id=0, has_side_effects=True, vmem_limit_bytes=VMEM_LIMIT
        ),
    )(etab, meta, nf, cot, wm, ws, adj)


def store_kernel(a_ref, b_ref, w_ref, oa_ref, ob_ref, om_ref, os_ref, sems):
    half = w_ref.shape[0] // 2
    copies = [
        pltpu.make_async_copy(src, dst, sems.at[i])
        for i, (src, dst) in enumerate(
            (
                (a_ref, oa_ref),
                (b_ref, ob_ref),
                (w_ref.at[pl.ds(0, half)], om_ref),
                (w_ref.at[pl.ds(half, half)], os_ref),
            )
        )
    ]
    for copy in copies:
        copy.start()
    for copy in copies:
        copy.wait()


def store(a, b, w):
    vmem = pl.BlockSpec(memory_space=pltpu.VMEM)
    hbm = pl.BlockSpec(memory_space=pl.ANY)
    piece = jax.ShapeDtypeStruct((w.shape[0] // 2, w.shape[1]), F32)
    return pl.pallas_call(
        store_kernel,
        name="store",
        out_shape=(
            jax.ShapeDtypeStruct(a.shape, a.dtype),
            jax.ShapeDtypeStruct(b.shape, b.dtype),
            piece,
            piece,
        ),
        in_specs=[vmem, vmem, vmem],
        out_specs=(hbm, hbm, hbm, hbm),
        scratch_shapes=[pltpu.SemaphoreType.DMA((4,))],
    )(a, b, w)


def by_slab(slots):
    rows = slots.reshape(NX, NZ, 2, 2).transpose(1, 0, 2, 3).reshape(NZ, CHUNK)
    return rows


def body(
    node_feat, cotangent, w_msg, w_self, adjacency, edge_src, edge_dst, send_src, recv_dst, live
):
    blocks = jnp.concatenate([by_slab(send_src), by_slab(recv_dst)], axis=0)
    blocks = jnp.pad(blocks, ((0, 0), (0, SLOTS - CHUNK)), constant_values=-1)
    slots = jnp.concatenate([edge_src.reshape(1, EDGES), edge_dst.reshape(1, EDGES)], axis=0)
    slots = jnp.pad(slots, ((0, 6), (0, SLOTS - EDGES)))
    row = lax.broadcasted_iota(I32, slots.shape, 0)
    slots = jnp.where(row == 2, live.reshape(1, 1), slots)
    meta, etab = tables(blocks, slots)
    adj = adjacency.reshape(-1, BLK, BLK)
    out, grad_feat, weights = layer(etab, meta, node_feat, cotangent, w_msg, w_self, adj)
    return store(out, grad_feat, weights)


def solution(mesh):
    in_specs = (
        P("edge", None),
        P("edge", None),
        P(),
        P(),
        P("edge", "feat", None, None, None),
        P("edge", "feat", None),
        P("edge", "feat", None),
        P("edge", "feat", None, None),
        P("edge", "feat", None, None),
        P("edge", "feat"),
    )
    out_specs = (P("edge", None), P("edge", None), P(), P())
    return jax.shard_map(body, mesh=mesh, in_specs=in_specs, out_specs=out_specs, check_vma=False)
```

time: 927 us -> 276 us (0.30)
  waiting for transfers between devices: 685 us -> 0 us
  Pallas kernels: 0 us -> 270 us
  other arithmetic: 63.8 us -> 1.36 us
  starting transfers between devices: 61.6 us -> 0 us
  blocking collectives: 52.7 us -> 0 us
  local copies, waits for them, and re-layouts: 37.4 us -> 2.55 us
  between operations: 15 us -> 1.31 us
  matrix products: 9.94 us -> 0 us
    all_to_all x5 -> x0, waiting for transfers between devices: 620 us -> none  [the longest x1 197 us: body(): lax.all_to_all(grad_partials.reshape(peer_count, send_slots, block_size,...]
    pallas_call x0 -> x3, Pallas kernels: none -> 270 us  [the longest x1 267 us: layer(): pl.pallas_call(layer_kernel, name='layer', out_shape=(jax.ShapeDtypeStruc...]
    all_gather x2 -> x0, waiting for transfers between devices: 65.1 us -> none  [over_pieces(): return lax.all_gather(value, axis).sum(0)]
    all_to_all x5 -> x0, starting transfers between devices: 61.5 us -> none  [the longest x1 19 us: body(): lax.all_to_all(partials.reshape(peer_count, dest_slots, block_size, hidde...]
    all_to_all x1 -> x0, blocking collectives: 52.7 us -> none  [sent_to_all(): lax.all_to_all(jnp.broadcast_to(value[None], (peers, *value.shape)), axis...]
    scatter-add x4 -> x0, other arithmetic: 46.5 us -> none  [the longest x1 17 us: body(): grad_owner = jnp.zeros((owned_blocks, block_size, hidden), jnp.float32).a...]
    gather x4 -> x0, local copies, waits for them, and re-layouts: 13.8 us -> none  [the longest x2 7.69 us: one_round(): jnp.take(source_rows, picks, axis=0)]
    unnamed x23 -> x0, local copies, waits for them, and re-layouts: 11.2 us -> none
  transfers between devices with their start and end apart: 7 -> 0, of which waited for: 6 -> 0; matrix products, arithmetic and copies ran while one was open for 3% -> 0% of each run, Pallas kernels for 0% -> 0%
where the time goes in v2:
time: 276 us
  Pallas kernels  270 us (98%)
    pallas_call x1, Pallas kernels, layer(): pl.pallas_call(layer_kernel, name='layer', out_shape=(jax.ShapeDtypeStruc...  267 us

profile of v2, /device:TPU:1, one launch (start us, length us, event | category | flops | bytes accessed | tf_op | source)
XLA Modules:
  0.0 275.6 jit_solution(14072399314592515101)
XLA Ops:
  1.3 0.7 pad_add_fusion.1
  2.0 0.7 pad_select_fusion.edges_ref
  2.6 0.8 reshape.29
  3.4 0.1 copy.18
  3.5 0.1 copy.20
  3.6 0.8 reshape.31
  4.4 0.1 copy.19
  4.5 0.1 copy.21
  4.6 0.6 pad.8.blocks_ref
  5.2 1.5 tables.1
  6.7 266.6 %layer.1 = (bf16[2048,128]{1,0:T(8,128)(2,1)}, bf16[2048,128]{1,0:T(8,128)(2,1)}, f32[256,128]{1,0:T(8,128)}) custom-call(s32[8,128]{1,0:T(8,128)} %get-tuple-element.9.etab, s32[8,8,128]{2,1,0:T(8,128)} %get-tuple-element.10.meta_ref, bf16[2048,128]{1,0:T(8,128)(2,1)} %nf_ref.1, bf16[2048,128]{1,0:T(8,128)(2,1)} %cot_ref.1, bf16[128,128]{1,0:T(8,128)(2,1)} %wm_ref.1, ...), custom_call_target="tpu_custom_call" | custom-call | tf_op jit(solution)/shard_map/layer/pallas_call | solution.py:521
  273.3 2.3 store.1
  (2 shorter events, 0.0 us)

commit v3 on v2

--- a/solution.py
+++ b/solution.py
@@ -13,6 +13,9 @@
 PEERS = 2 * NX
 VMEM_LIMIT = 60 * 1024 * 1024
 GROUP = 8
+NH = 2
+PIECE = BLK // NH
+NT = NZ * NH
 SLAB = NX * NY * 2
 CHUNK = 2 * PEERS
 EDGES = 64
@@ -141,7 +144,9 @@
     def project(i):
         b = (QTR * y + i) % OWN
         node = nf_ref[pl.ds(pl.multiple_of(b * BLK, BLK), BLK)]
-        dense[z, b] = dot(node, wm_ref[...], ((1,), (0,))).astype(BF16)
+        message = dot(node, wm_ref[...], ((1,), (0,))).astype(BF16)
+        for h in range(NH):
+            dense[z, h, b] = message[h * PIECE : (h + 1) * PIECE]
 
     loop(0, OWN, project)
     pl.semaphore_wait(barrier, len(peers))
@@ -151,6 +156,9 @@
 
     def gather(forward):
         block_row = SRC if forward else DST
+
+        def source_of(t):
+            return (z + NZ - zoff(t // NH)) % NZ
 
         def mcopy(d):
             return remote(
@@ -158,123 +166,143 @@
                 device(x, y, (z + d) % NZ, c),
             )
 
-        def zcopy(d):
-            part = dense.at[z, own]
-            return remote(part, part, g_zs.at[d], g_zr.at[d], device(x, y, (z + d) % NZ, c))
-
-        def ycopy(k, zi, d):
-            part = dense.at[zi, own]
-            return remote(part, part, g_ys.at[k, d], g_yr.at[k, d], device(x, (y + d) % NY, z, c))
-
-        def xcopy(k, zi, j):
+        def zcopy(zi, h, d, step):
+            part = dense.at[zi, h, own]
+            at = d * NH + h
+            return remote(part, part, g_zs.at[at], g_zr.at[at], device(x, y, (z + NZ + step) % NZ, c))
+
+        def ycopy(t, d):
+            part = dense.at[source_of(t), t % NH, own]
+            return remote(part, part, g_ys.at[t, d], g_yr.at[t, d], device(x, (y + d) % NY, z, c))
+
+        def xcopy(t, j):
             px, pc = slab_peer(x, c, j)
+            zi = source_of(t)
             return remote(
-                staged.at[px * 2 + pc, zi], rows.at[slots_of(x, zi, c)], g_xs.at[k, j], g_xr.at[k, j],
-                device(px, y, z, pc),
+                staged.at[px * 2 + pc, zi, t % NH], rows.at[slots_of(x, zi, c), t % NH],
+                g_xs.at[t, j], g_xr.at[t, j], device(px, y, z, pc),
             )
 
         def meta_load(k, zi):
             return pltpu.make_async_copy(meta_in.at[zi], meta.at[zi], ml.at[k])
 
-        def spread(k):
+        def spread(t):
+            k, h = t // NH, t % NH
             d = zoff(k)
-            zi = (z + NZ - d) % NZ
-            part = dense.at[zi, own]
+            zi = source_of(t)
             if forward:
-                remote(meta_ref.at[z], meta_in.at[zi], ms.at[d], mr.at[d], here).wait_recv()
-                meta_load(k, zi).start()
-            remote(part, part, g_zs.at[d], g_zr.at[d], here).wait_recv()
+
+                @pl.when(h == 0)
+                def _():
+                    remote(meta_ref.at[z], meta_in.at[zi], ms.at[d], mr.at[d], here).wait_recv()
+                    meta_load(k, zi).start()
+
+            part = dense.at[zi, h, own]
+            at = d * NH + h
+            remote(part, part, g_zs.at[at], g_zr.at[at], here).wait_recv()
+
+            @pl.when(k < NZ - 2)
+            def _():
+                step = 2 * (k % 2) - 1
+                zcopy(zi, h, (d + NZ + step) % NZ, step).start()
+
             for dy in (1, 3, 2):
-                ycopy(k, zi, dy).start()
-
-        def collect(k):
-            zi = (z + NZ - zoff(k)) % NZ
+                ycopy(t, dy).start()
+
+        def collect(t):
+            zi = source_of(t)
             for dy in (1, 3, 2):
-                part = dense.at[zi, pl.ds(QTR * ((y + NY - dy) % NY), QTR)]
-                remote(part, part, g_ys.at[k, dy], g_yr.at[k, dy], here).wait_recv()
+                part = dense.at[zi, t % NH, pl.ds(QTR * ((y + NY - dy) % NY), QTR)]
+                remote(part, part, g_ys.at[t, dy], g_yr.at[t, dy], here).wait_recv()
             if forward:
-                meta_load(k, zi).wait()
-
-        def deliver(k):
-            zi = (z + NZ - zoff(k)) % NZ
-            chunk[...] = dense[zi]
+
+                @pl.when(t % NH == 0)
+                def _():
+                    meta_load(t // NH, zi).wait()
+
+        def deliver(t):
+            zi, h = source_of(t), t % NH
+            chunk[...] = dense[zi, h]
 
             def pick(j):
                 px, pc = slab_peer(x, c, j)
                 pid = px * 2 + pc
                 for s in range(2):
-                    staged[pid, zi, s] = chunk[meta[zi, block_row, pid * 2 + s]]
+                    staged[pid, zi, h, s] = chunk[meta[zi, block_row, pid * 2 + s]]
 
             loop(1, PEERS, pick)
             base = ((x * NZ + zi) * 2 + c) * 2
             for s in range(2):
-                rows[base + s] = chunk[meta[zi, block_row, me * 2 + s]]
-            loop(1, PEERS, lambda j: xcopy(k, zi, j).start())
-
-        for d in (1, 7, 2, 6, 3, 5, 4):
-            if forward:
+                rows[base + s, h] = chunk[meta[zi, block_row, me * 2 + s]]
+            loop(1, PEERS, lambda j: xcopy(t, j).start())
+
+        for h in range(NH):
+            for d, step in ((1, 1), (NZ - 1, -1)):
+                zcopy(z, h, d, step).start()
+        if forward:
+            for d in (1, 7, 2, 6, 3, 5, 4):
                 mcopy(d).start()
-            zcopy(d).start()
-        if forward:
             own_meta.wait()
-            deliver(0)
-            spread(1)
+            loop(0, NH, deliver)
+            loop(NH, 2 * NH, spread)
         else:
-            for dy in (1, 3, 2):
-                ycopy(0, z, dy).start()
-            spread(1)
-            collect(0)
-            deliver(0)
-
-        def step(k):
-            @pl.when(k < NZ - 1)
+            for h in range(NH):
+                for dy in (1, 3, 2):
+                    ycopy(h, dy).start()
+
+        def step(t):
+            @pl.when(t < NH * (NZ - 1))
             def _():
-                spread(k + 1)
-
-            collect(k)
-            deliver(k)
-
-        loop(1, NZ, step)
+                spread(t + NH)
+
+            collect(t)
+            deliver(t)
+
+        loop(NH if forward else 0, NH * NZ, step)
 
         for d in range(1, NZ):
             if forward:
                 mcopy(d).wait_send()
-            zcopy(d).wait_send()
-
-        def finish(k):
-            zi = (z + NZ - zoff(k)) % NZ
+            for h in range(NH):
+                zcopy(z, h, d, 1).wait_send()
+
+        def finish(t):
+            zi = source_of(t)
 
             def each(j):
-                xcopy(k, zi, j).wait_send()
+                xcopy(t, j).wait_send()
                 sx, sc = slab_source(x, c, j)
                 remote(
-                    staged.at[me, zi], rows.at[slots_of(sx, zi, sc)], g_xs.at[k, j], g_xr.at[k, j], here
+                    staged.at[me, zi, t % NH], rows.at[slots_of(sx, zi, sc), t % NH],
+                    g_xs.at[t, j], g_xr.at[t, j], here,
                 ).wait_recv()
 
             loop(1, PEERS, each)
 
-        loop(0, NZ, finish)
-
-        def sent(k):
-            zi = (z + NZ - zoff(k)) % NZ
+        loop(0, NH * NZ, finish)
+
+        def sent(t):
             for dy in range(1, NY):
-                ycopy(k, zi, dy).wait_send()
-
-        loop(1 if forward else 0, NZ, sent)
+                ycopy(t, dy).wait_send()
+
+        loop(NH if forward else 0, NH * NZ, sent)
+
+    def whole(pieces):
+        return pieces.reshape(BLK, pieces.shape[-1])
 
     def edges(forward):
         pick, prev = (SRC, DST_PREV) if forward else (DST, SRC_PREV)
         contract = ((1,), (0,)) if forward else ((0,), (0,))
-        chain[EDGES] = jnp.zeros((BLK, BLK), F32)
+        chain[EDGES] = jnp.zeros(chain.shape[1:], F32)
 
         def one_round(r):
             terms = []
             for i in range(GROUP):
                 k = r * GROUP + i
-                terms.append(dot(adj[k], rows[etab[pick, k]], contract))
+                terms.append(dot(adj[k], whole(rows[etab[pick, k]]), contract))
             for i in range(GROUP):
                 k = r * GROUP + i
-                chain[k] = terms[i] + chain[etab[prev, k]]
+                chain[k] = terms[i].reshape(chain.shape[1:]) + chain[etab[prev, k]]
 
         loop(0, EDGES // GROUP, one_round)
 
@@ -282,122 +310,127 @@
         end = DST_LAST if forward else SRC_LAST
         run_prev, run_last = (DST_PREV, DST_LAST) if forward else (SRC_PREV, SRC_LAST)
 
-        def owner(k):
-            return (z + zoff(NZ - 1 - k)) % NZ
-
-        def xcopy(k, j):
-            zi = owner(k)
+        def owner(t):
+            return (z + zoff(NZ - 1 - t // NH)) % NZ
+
+        def xcopy(t, j):
+            zi, h = owner(t), t % NH
             px, pc = slab_peer(x, c, j)
             return remote(
-                parts.at[slots_of(px, zi, pc)], arrived.at[zi, pl.ds(2 * me, 2)],
-                s_xs.at[k, j], s_xr.at[k, j], device(px, y, z, pc),
+                parts.at[slots_of(px, zi, pc), h], arrived.at[zi, h, pl.ds(2 * me, 2)],
+                s_xs.at[t, j], s_xr.at[t, j], device(px, y, z, pc),
             )
 
-        def local(k):
-            zi = owner(k)
+        def local(t):
+            zi, h = owner(t), t % NH
             return pltpu.make_async_copy(
-                parts.at[slots_of(x, zi, c)], arrived.at[zi, pl.ds(2 * me, 2)], ls.at[k]
+                parts.at[slots_of(x, zi, c), h], arrived.at[zi, h, pl.ds(2 * me, 2)], ls.at[t]
             )
 
-        def ycopy(k, d):
+        def ycopy(t, d):
             return remote(
-                ysend.at[k, d - 1], yrecv.at[k, d - 1], s_ys.at[k, d], s_yr.at[k, d],
+                ysend.at[t, d - 1], yrecv.at[t, d - 1], s_ys.at[t, d], s_yr.at[t, d],
                 device(x, (y + d) % NY, z, c),
             )
 
-        def zcopy(d):
+        def zcopy(d, h):
+            at = d * NH + h
             return remote(
-                zsend.at[d - 1], zrecv.at[d - 1], s_zs.at[d], s_zr.at[d], device(x, y, (z + d) % NZ, c)
+                zsend.at[d - 1, h], zrecv.at[d - 1, h], s_zs.at[at], s_zr.at[at],
+                device(x, y, (z + d) % NZ, c),
             )
 
-        def write(k):
-            zi = owner(k)
+        def write(t):
+            zi, h = owner(t), t % NH
 
             def each(pid):
                 base = (((pid // 2) * NZ + zi) * 2 + pid % 2) * 2
                 for s in range(2):
-                    parts[base + s] = chain[etab[end, base + s]].astype(BF16)
+                    parts[base + s, h] = chain[etab[end, base + s], h].astype(BF16)
 
             loop(0, PEERS, each)
 
-        def push(k):
-            local(k).start()
-            loop(1, PEERS, lambda j: xcopy(k, j).start())
+        def push(t):
+            local(t).start()
+            loop(1, PEERS, lambda j: xcopy(t, j).start())
 
         write(0)
 
-        def issue(k):
-            write(k)
-            push(k - 1)
-
-        loop(1, NZ, issue)
-        push(NZ - 1)
-
-        runs[CHUNK] = jnp.zeros((BLK, BLK), F32)
-
-        def merge(k):
-            zi = owner(k)
-            local(k).wait()
+        def issue(t):
+            write(t)
+            push(t - 1)
+
+        loop(1, NH * NZ, issue)
+        push(NH * NZ - 1)
+
+        runs[CHUNK] = jnp.zeros(runs.shape[1:], F32)
+
+        def merge(t):
+            zi, h = owner(t), t % NH
+            local(t).wait()
 
             def each(j):
                 sx, sc = slab_source(x, c, j)
                 remote(
-                    parts.at[slots_of(x, zi, c)], arrived.at[zi, pl.ds(2 * (sx * 2 + sc), 2)],
-                    s_xs.at[k, j], s_xr.at[k, j], here,
+                    parts.at[slots_of(x, zi, c), h], arrived.at[zi, h, pl.ds(2 * (sx * 2 + sc), 2)],
+                    s_xs.at[t, j], s_xr.at[t, j], here,
                 ).wait_recv()
 
             loop(1, PEERS, each)
 
             def run(i):
-                runs[i] = arrived[zi, i].astype(F32) + runs[meta[zi, run_prev, i]]
+                runs[i] = arrived[zi, h, i].astype(F32) + runs[meta[zi, run_prev, i]]
 
             loop(0, CHUNK, run)
             for d in (1, 3, 2):
                 base = QTR * ((y + d) % NY)
                 for b in range(QTR):
-                    ysend[k, d - 1, b] = runs[meta[zi, run_last, base + b]].astype(BF16)
-                ycopy(k, d).start()
+                    ysend[t, d - 1, b] = runs[meta[zi, run_last, base + b]].astype(BF16)
+                ycopy(t, d).start()
             for b in range(QTR):
-                yown[k, b] = runs[meta[zi, run_last, QTR * y + b]]
-
-        def total_of(k):
+                yown[t, b] = runs[meta[zi, run_last, QTR * y + b]]
+
+        def total_of(t):
             for d in range(1, NY):
-                ycopy(k, d).wait_recv()
+                ycopy(t, d).wait_recv()
             return [
-                yown[k, b] + yrecv[k, 0, b].astype(F32) + yrecv[k, 1, b].astype(F32)
-                + yrecv[k, 2, b].astype(F32)
+                yown[t, b] + yrecv[t, 0, b].astype(F32) + yrecv[t, 1, b].astype(F32)
+                + yrecv[t, 2, b].astype(F32)
                 for b in range(QTR)
             ]
 
-        def pass_on(k):
-            d = zoff(NZ - 1 - k)
-            for b, value in enumerate(total_of(k)):
-                zsend[d - 1, b] = value.astype(BF16)
-            zcopy(d).start()
-
-        merge(0)
-
-        def step(k):
-            merge(k)
-            pass_on(k - 1)
-
-        loop(1, NZ, step)
-        for b, value in enumerate(total_of(NZ - 1)):
-            total[b] = value
+        def pass_on(t):
+            d, h = zoff(NZ - 1 - t // NH), t % NH
+            for b, value in enumerate(total_of(t)):
+                zsend[d - 1, h, b] = value.astype(BF16)
+            zcopy(d, h).start()
+
+        loop(0, NH, merge)
+
+        def step(t):
+            merge(t)
+            pass_on(t - NH)
+
+        loop(NH, NH * NZ, step)
+        for h in range(NH):
+            for b, value in enumerate(total_of(NH * (NZ - 1) + h)):
+                total[b, h] = value
         for d in (1, 7, 2, 6, 3, 5, 4):
-            zcopy(d).wait_recv()
-            for b in range(QTR):
-                total[b] += zrecv[d - 1, b].astype(F32)
+            for h in range(NH):
+                zcopy(d, h).wait_recv()
+                for b in range(QTR):
+                    total[b, h] += zrecv[d - 1, h, b].astype(F32)
 
         for d in range(1, NZ):
-            zcopy(d).wait_send()
-
-        def finish(k):
+            for h in range(NH):
+                zcopy(d, h).wait_send()
+
+        def finish(t):
             for d in range(1, NY):
-                ycopy(k, d).wait_send()
-            loop(1, PEERS, lambda j: xcopy(k, j).wait_send())
-
-        loop(0, NZ, finish)
+                ycopy(t, d).wait_send()
+            loop(1, PEERS, lambda j: xcopy(t, j).wait_send())
+
+        loop(0, NH * NZ, finish)
 
     def share(i, d):
         part = (out_ref, gf_ref)[i].at[mine_rows]
@@ -419,13 +452,14 @@
 
     def activate(b):
         node = nf_ref[block_rows(b)]
-        preact = dot(node, ws_ref[...], ((1,), (0,))) + total[b]
+        preact = dot(node, ws_ref[...], ((1,), (0,))) + whole(total[b])
         sig = jax.nn.sigmoid(preact)
         out_ref[block_rows(b)] = (preact * sig).astype(BF16)
         grad = cot_ref[block_rows(b)].astype(F32) * sig * (1.0 + preact * (1.0 - sig))
         grad = grad.astype(BF16)
         pre[b] = grad
-        dense[z, QTR * y + b] = grad
+        for h in range(NH):
+            dense[z, h, QTR * y + b] = grad[h * PIECE : (h + 1) * PIECE]
 
     def outer(at, b, value):
         term = dot(nf_ref[block_rows(b)], value, ((0,), (0,)))
@@ -446,7 +480,7 @@
     scatter(False)
 
     for b in range(QTR):
-        outer(0, b, total[b].astype(BF16))
+        outer(0, b, whole(total[b]).astype(BF16))
 
     height = 2 * BLK // SLAB
     slab_me = (x * NY + y) * 2 + c
@@ -479,7 +513,7 @@
     for b in range(QTR):
         gf_ref[block_rows(b)] = (
             dot(pre[b], ws_ref[...], ((1,), (1,)))
-            + dot(total[b].astype(BF16), wm_ref[...], ((1,), (1,)))
+            + dot(whole(total[b]).astype(BF16), wm_ref[...], ((1,), (1,)))
         ).astype(BF16)
     for d in (1, 3, 2):
         share(1, d).start()
@@ -516,7 +550,7 @@
     dma = pltpu.SemaphoreType.DMA
     vmem = pl.BlockSpec(memory_space=pltpu.VMEM)
     hidden = nf.shape[1]
-    block = (BLK, hidden)
+    block, piece = (BLK, hidden), (PIECE, hidden)
     height = 2 * BLK // SLAB
     return pl.pallas_call(
         layer_kernel,
@@ -532,20 +566,20 @@
             pltpu.VMEM((NZ, 8, SLOTS), I32),
             pltpu.SMEM((NZ, 8, SLOTS), I32),
             pltpu.VMEM((EDGES, BLK, BLK), BF16),
-            pltpu.VMEM((NZ, OWN, *block), BF16),
-            pltpu.VMEM((OWN, *block), BF16),
-            pltpu.VMEM((PEERS, NZ, 2, *block), BF16),
-            pltpu.VMEM((SLOTS, *block), BF16),
-            pltpu.VMEM((EDGES + 1, *block), F32),
-            pltpu.VMEM((SLOTS, *block), BF16),
-            pltpu.VMEM((NZ, CHUNK, *block), BF16),
-            pltpu.VMEM((CHUNK + 1, *block), F32),
-            pltpu.VMEM((NZ, NY - 1, QTR, *block), BF16),
-            pltpu.VMEM((NZ, QTR, *block), F32),
-            pltpu.VMEM((NZ, NY - 1, QTR, *block), BF16),
-            pltpu.VMEM((NZ - 1, QTR, *block), BF16),
-            pltpu.VMEM((NZ - 1, QTR, *block), BF16),
-            pltpu.VMEM((QTR, *block), F32),
+            pltpu.VMEM((NZ, NH, OWN, *piece), BF16),
+            pltpu.VMEM((OWN, *piece), BF16),
+            pltpu.VMEM((PEERS, NZ, NH, 2, *piece), BF16),
+            pltpu.VMEM((SLOTS, NH, *piece), BF16),
+            pltpu.VMEM((EDGES + 1, NH, *piece), F32),
+            pltpu.VMEM((SLOTS, NH, *piece), BF16),
+            pltpu.VMEM((NZ, NH, CHUNK, *piece), BF16),
+            pltpu.VMEM((CHUNK + 1, *piece), F32),
+            pltpu.VMEM((NT, NY - 1, QTR, *piece), BF16),
+            pltpu.VMEM((NT, QTR, *piece), F32),
+            pltpu.VMEM((NT, NY - 1, QTR, *piece), BF16),
+            pltpu.VMEM((NZ - 1, NH, QTR, *piece), BF16),
+            pltpu.VMEM((NZ - 1, NH, QTR, *piece), BF16),
+            pltpu.VMEM((QTR, NH, *piece), F32),
             pltpu.VMEM((QTR, *block), BF16),
             pltpu.VMEM((2 * hidden, hidden), F32),
             pltpu.VMEM((SLAB, height, hidden), F32),
@@ -555,19 +589,19 @@
             dma((NZ,)),
             dma((NZ,)),
             dma((NZ,)),
-            dma((NZ,)),
-            dma((NZ,)),
-            dma((NZ, NY)),
-            dma((NZ, NY)),
-            dma((NZ, PEERS)),
-            dma((NZ, PEERS)),
-            dma((NZ,)),
-            dma((NZ, PEERS)),
-            dma((NZ, PEERS)),
-            dma((NZ, NY)),
-            dma((NZ, NY)),
-            dma((NZ,)),
-            dma((NZ,)),
+            dma((NT,)),
+            dma((NT,)),
+            dma((NT, NY)),
+            dma((NT, NY)),
+            dma((NT, PEERS)),
+            dma((NT, PEERS)),
+            dma((NT,)),
+            dma((NT, PEERS)),
+            dma((NT, PEERS)),
+            dma((NT, NY)),
+            dma((NT, NY)),
+            dma((NT,)),
+            dma((NT,)),
             dma((2, NY)),
             dma((2, NY)),
             dma((SLAB,)),

time: 276 us -> 269 us (0.975)
  Pallas kernels: 270 us -> 264 us
    pallas_call x1, Pallas kernels: 267 us -> 260 us  [layer(): pl.pallas_call(layer_kernel, name='layer', out_shape=(jax.ShapeDtypeStruc...]
where the time goes in v3:
time: 269 us
  Pallas kernels  264 us (98%)
    pallas_call x1, Pallas kernels, layer(): pl.pallas_call(layer_kernel, name='layer', out_shape=(jax.ShapeDtypeStruc...  260 us

profile of v3, /device:TPU:1, one launch (start us, length us, event | category | flops | bytes accessed | tf_op | source)
XLA Modules:
  0.0 269.0 jit_solution(13551759033809459735)
XLA Ops:
  1.3 0.7 pad_add_fusion.1
  2.0 0.7 pad_select_fusion.edges_ref
  2.6 0.8 reshape.29
  3.4 0.1 copy.18
  3.5 0.1 copy.20
  3.6 0.8 reshape.31
  4.4 0.1 copy.19
  4.5 0.1 copy.21
  4.6 0.6 pad.8.blocks_ref
  5.2 1.5 tables.1
  6.7 260.0 %layer.1 = (bf16[2048,128]{1,0:T(8,128)(2,1)}, bf16[2048,128]{1,0:T(8,128)(2,1)}, f32[256,128]{1,0:T(8,128)}) custom-call(s32[8,128]{1,0:T(8,128)} %get-tuple-element.9.etab, s32[8,8,128]{2,1,0:T(8,128)} %get-tuple-element.10.meta_ref, bf16[2048,128]{1,0:T(8,128)(2,1)} %nf_ref.1, bf16[2048,128]{1,0:T(8,128)(2,1)} %cot_ref.1, bf16[128,128]{1,0:T(8,128)(2,1)} %wm_ref.1, ...), custom_call_target="tpu_custom_call" | custom-call | tf_op jit(solution)/shard_map/layer/pallas_call | solution.py:555
  266.8 2.3 store.1
  (2 shorter events, 0.0 us)

commit v4 on v3

--- a/solution.py
+++ b/solution.py
@@ -68,31 +68,46 @@
     return lax.dot_general(a, b, (contract, ((), ())), preferred_element_type=F32)
 
 
-def tables_kernel(blocks_ref, edges_ref, meta_ref, etab_ref):
-    shape = blocks_ref.shape
-    blocks = blocks_ref[...]
-    lane = lax.broadcasted_iota(I32, shape, 1)
-    prev = jnp.full(shape, CHUNK, I32)
-    for d in range(CHUNK - 1, 0, -1):
-        same = (pltpu.roll(blocks, d, 1) == blocks) & (lane >= d) & (lane < CHUNK)
-        prev = jnp.where(same, lane - d, prev)
-    last = jnp.full(shape, CHUNK, I32)
-    for i in range(CHUNK):
-        last = jnp.where(blocks[:, i : i + 1] == lane, i, last)
-    for row, (value, at) in enumerate(
-        ((blocks, 0), (prev, 0), (last, 0), (blocks, NZ), (prev, NZ), (last, NZ))
-    ):
-        for z in range(NZ):
-            meta_ref[z, row : row + 1] = value[at + z : at + z + 1]
-
+def tables_kernel(send_ref, recv_ref, src_ref, dst_ref, live_ref, meta_ref, etab_ref, pad):
+    shape = pad.shape[1:]
+    for s in range(2):
+        pad[s] = jnp.zeros(shape, I32)
+        pad[s, 0:1, 0:EDGES] = send_ref[s : s + 1, :]
+        pad[s, 1:2, 0:EDGES] = recv_ref[s : s + 1, :]
     wide = (SLOTS, SLOTS)
     down = lax.broadcasted_iota(I32, wide, 0)
     along = lax.broadcasted_iota(I32, wide, 1)
+    peer = (along % CHUNK) // 2
+    edge = ((peer // 2) * NZ + along // CHUNK) * 2 + peer % 2
+    found = jnp.zeros(shape, F32)
+    for s in range(2):
+        pick = jnp.where((down == edge) & (along % 2 == s), 1.0, 0.0).astype(BF16)
+        found += dot(pad[s].astype(F32).astype(BF16), pick, ((1,), (0,)))
+    blocks = found.astype(I32)
+    spot = lax.broadcasted_iota(I32, shape, 1) % CHUNK
+    prev = jnp.full(shape, CHUNK, I32)
+    for d in range(CHUNK - 1, 0, -1):
+        same = (pltpu.roll(blocks, d, 1) == blocks) & (spot >= d)
+        prev = jnp.where(same, spot - d, prev)
+    last = jnp.full(shape, -1, I32)
+    for t in range(1 - CHUNK, CHUNK):
+        other = blocks if t == 0 else pltpu.roll(blocks, (SLOTS - t) % SLOTS, 1)
+        at = spot + t
+        last = jnp.where((other == spot) & (at >= 0) & (at < CHUNK), at, last)
+    last = jnp.where(last < 0, CHUNK, last)
+    meta_ref[...] = jnp.zeros(shape, I32)
+    for i in range(2):
+        for row, value in enumerate((blocks, prev, last)):
+            meta_ref[3 * i + row : 3 * i + row + 1] = value[i : i + 1]
+
+    pad[0] = jnp.zeros(shape, I32)
+    pad[0, 0:1, 0:EDGES] = src_ref[...]
+    pad[0, 1:2, 0:EDGES] = dst_ref[...]
     downf, alongf = down.astype(F32), along.astype(F32)
-    live = edges_ref[2:3, :]
+    live = live_ref[0, 0]
     none = float(EDGES)
     for row, prev_row, last_row in ((0, SRC_PREV, SRC_LAST), (1, DST_PREV, DST_LAST)):
-        slot = edges_ref[row : row + 1, :]
+        slot = pad[0, row : row + 1, :]
         etab_ref[(SRC, DST)[row] : (SRC, DST)[row] + 1] = slot
         on = lax.broadcasted_iota(I32, slot.shape, 1) < live
         flat = jnp.where(on, slot.astype(F32), -1.0)
@@ -104,23 +119,28 @@
         etab_ref[last_row : last_row + 1] = jnp.where(ends < 0.0, none, ends).astype(I32)
 
 
-def tables(blocks, edges):
+def tables(send, recv, src, dst, live):
+    vmem = pl.BlockSpec(memory_space=pltpu.VMEM)
     return pl.pallas_call(
         tables_kernel,
         name="tables",
         out_shape=(
-            jax.ShapeDtypeStruct((NZ, 8, SLOTS), I32),
+            jax.ShapeDtypeStruct((8, SLOTS), I32),
             jax.ShapeDtypeStruct((8, SLOTS), I32),
         ),
-    )(blocks, edges)
+        in_specs=[vmem, vmem, vmem, vmem, pl.BlockSpec(memory_space=pltpu.SMEM)],
+        out_specs=(vmem, vmem),
+        scratch_shapes=[pltpu.VMEM((2, 8, SLOTS), I32)],
+    )(send, recv, src, dst, live)
 
 
 def layer_kernel(
-    etab, meta_ref, nf_ref, cot_ref, wm_ref, ws_ref, adj_ref,
+    etab_in, meta_ref, nf_in, cot_in, wm_in, ws_in, adj_in,
     out_ref, gf_ref, ow_ref,
+    etab, nf_ref, cot_ref, wm_ref, ws_ref,
     meta_in, meta, adj, dense, chunk, staged, rows, chain, parts, arrived, runs,
     ysend, yown, yrecv, zsend, zrecv, total, pre, weights, first, mine, second,
-    al, ml, ms, mr, g_zs, g_zr, g_ys, g_yr, g_xs, g_xr,
+    ins, ml, ms, mr, g_zs, g_zr, g_ys, g_yr, g_xs, g_xr,
     ls, s_xs, s_xr, s_ys, s_yr, s_zs, s_zr, gs, gr, s1, r1, s2, r2, s3, r3,
 ):
     x, y, z, c = place()
@@ -130,16 +150,32 @@
     mine_rows = pl.ds(quarter * y, quarter)
     own = pl.ds(QTR * y, QTR)
 
+    fetches = [
+        pltpu.make_async_copy(src, dst, ins.at[i])
+        for i, (src, dst) in enumerate(
+            (
+                (nf_in, nf_ref),
+                (wm_in, wm_ref),
+                (ws_in, ws_ref),
+                (cot_in.at[mine_rows], cot_ref),
+                (etab_in, etab),
+                (adj_in, adj),
+            )
+        )
+    ]
+    own_meta = pltpu.make_async_copy(meta_ref, meta.at[z], ml.at[0])
+    for fetch in fetches[:2]:
+        fetch.start()
+    own_meta.start()
     barrier = pltpu.get_barrier_semaphore()
     peers = [slab_device(x, y, z, c, j) for j in range(1, SLAB)]
     peers += [device(x, y, (z + d) % NZ, c) for d in range(1, NZ)]
     for peer in peers:
         pl.semaphore_signal(barrier, inc=1, device_id=peer, device_id_type=MESH)
-
-    adj_copy = pltpu.make_async_copy(adj_ref, adj, al)
-    adj_copy.start()
-    own_meta = pltpu.make_async_copy(meta_ref.at[z], meta.at[z], ml.at[0])
-    own_meta.start()
+    for fetch in fetches[2:]:
+        fetch.start()
+    for fetch in fetches[:2]:
+        fetch.wait()
 
     def project(i):
         b = (QTR * y + i) % OWN
@@ -162,7 +198,7 @@
 
         def mcopy(d):
             return remote(
-                meta_ref.at[(z + d) % NZ], meta_in.at[z], ms.at[d], mr.at[d],
+                meta_ref, meta_in.at[z], ms.at[d], mr.at[d],
                 device(x, y, (z + d) % NZ, c),
             )
 
@@ -194,7 +230,7 @@
 
                 @pl.when(h == 0)
                 def _():
-                    remote(meta_ref.at[z], meta_in.at[zi], ms.at[d], mr.at[d], here).wait_recv()
+                    remote(meta_ref, meta_in.at[zi], ms.at[d], mr.at[d], here).wait_recv()
                     meta_load(k, zi).start()
 
             part = dense.at[zi, h, own]
@@ -228,12 +264,12 @@
                 px, pc = slab_peer(x, c, j)
                 pid = px * 2 + pc
                 for s in range(2):
-                    staged[pid, zi, h, s] = chunk[meta[zi, block_row, pid * 2 + s]]
+                    staged[pid, zi, h, s] = chunk[meta[zi, block_row, CHUNK * z + pid * 2 + s]]
 
             loop(1, PEERS, pick)
             base = ((x * NZ + zi) * 2 + c) * 2
             for s in range(2):
-                rows[base + s, h] = chunk[meta[zi, block_row, me * 2 + s]]
+                rows[base + s, h] = chunk[meta[zi, block_row, CHUNK * z + me * 2 + s]]
             loop(1, PEERS, lambda j: xcopy(t, j).start())
 
         for h in range(NH):
@@ -379,16 +415,16 @@
             loop(1, PEERS, each)
 
             def run(i):
-                runs[i] = arrived[zi, h, i].astype(F32) + runs[meta[zi, run_prev, i]]
+                runs[i] = arrived[zi, h, i].astype(F32) + runs[meta[zi, run_prev, CHUNK * z + i]]
 
             loop(0, CHUNK, run)
             for d in (1, 3, 2):
                 base = QTR * ((y + d) % NY)
                 for b in range(QTR):
-                    ysend[t, d - 1, b] = runs[meta[zi, run_last, base + b]].astype(BF16)
+                    ysend[t, d - 1, b] = runs[meta[zi, run_last, CHUNK * z + base + b]].astype(BF16)
                 ycopy(t, d).start()
             for b in range(QTR):
-                yown[t, b] = runs[meta[zi, run_last, QTR * y + b]]
+                yown[t, b] = runs[meta[zi, run_last, CHUNK * z + QTR * y + b]]
 
         def total_of(t):
             for d in range(1, NY):
@@ -446,7 +482,8 @@
         return pl.ds(pl.multiple_of((QTR * y + b) * BLK, BLK), BLK)
 
     gather(True)
-    adj_copy.wait()
+    for fetch in fetches[2:]:
+        fetch.wait()
     edges(True)
     scatter(True)
 
@@ -455,7 +492,7 @@
         preact = dot(node, ws_ref[...], ((1,), (0,))) + whole(total[b])
         sig = jax.nn.sigmoid(preact)
         out_ref[block_rows(b)] = (preact * sig).astype(BF16)
-        grad = cot_ref[block_rows(b)].astype(F32) * sig * (1.0 + preact * (1.0 - sig))
+        grad = cot_ref[BLK * b : BLK * (b + 1)].astype(F32) * sig * (1.0 + preact * (1.0 - sig))
         grad = grad.astype(BF16)
         pre[b] = grad
         for h in range(NH):
@@ -560,9 +597,14 @@
             jax.ShapeDtypeStruct(nf.shape, BF16),
             jax.ShapeDtypeStruct((2 * hidden, hidden), F32),
         ),
-        in_specs=[pl.BlockSpec(memory_space=pltpu.SMEM), vmem, vmem, vmem, vmem, vmem, pl.BlockSpec(memory_space=pl.ANY)],
+        in_specs=[pl.BlockSpec(memory_space=pl.ANY)] * 7,
         out_specs=(vmem, vmem, vmem),
         scratch_shapes=[
+            pltpu.SMEM((8, SLOTS), I32),
+            pltpu.VMEM(nf.shape, BF16),
+            pltpu.VMEM((nf.shape[0] // NY, hidden), BF16),
+            pltpu.VMEM(wm.shape, BF16),
+            pltpu.VMEM(ws.shape, BF16),
             pltpu.VMEM((NZ, 8, SLOTS), I32),
             pltpu.SMEM((NZ, 8, SLOTS), I32),
             pltpu.VMEM((EDGES, BLK, BLK), BF16),
@@ -585,7 +627,7 @@
             pltpu.VMEM((SLAB, height, hidden), F32),
             pltpu.VMEM((2, height, hidden), F32),
             pltpu.VMEM((NZ, height, hidden), F32),
-            dma,
+            dma((6,)),
             dma((NZ,)),
             dma((NZ,)),
             dma((NZ,)),
@@ -655,21 +697,11 @@
     )(a, b, w)
 
 
-def by_slab(slots):
-    rows = slots.reshape(NX, NZ, 2, 2).transpose(1, 0, 2, 3).reshape(NZ, CHUNK)
-    return rows
-
-
 def body(
     node_feat, cotangent, w_msg, w_self, adjacency, edge_src, edge_dst, send_src, recv_dst, live
 ):
-    blocks = jnp.concatenate([by_slab(send_src), by_slab(recv_dst)], axis=0)
-    blocks = jnp.pad(blocks, ((0, 0), (0, SLOTS - CHUNK)), constant_values=-1)
-    slots = jnp.concatenate([edge_src.reshape(1, EDGES), edge_dst.reshape(1, EDGES)], axis=0)
-    slots = jnp.pad(slots, ((0, 6), (0, SLOTS - EDGES)))
-    row = lax.broadcasted_iota(I32, slots.shape, 0)
-    slots = jnp.where(row == 2, live.reshape(1, 1), slots)
-    meta, etab = tables(blocks, slots)
+    send, recv = send_src.reshape(-1, 2).T, recv_dst.reshape(-1, 2).T
+    meta, etab = tables(send, recv, edge_src.reshape(1, -1), edge_dst.reshape(1, -1), live)
     adj = adjacency.reshape(-1, BLK, BLK)
     out, grad_feat, weights = layer(etab, meta, node_feat, cotangent, w_msg, w_self, adj)
     return store(out, grad_feat, weights)

time: 269 us -> 264 us (0.981)
  no operation moved by 1% of the time
where the time goes in v4:
time: 264 us
  Pallas kernels  263 us (100%)
    pallas_call x1, Pallas kernels, layer(): pl.pallas_call(layer_kernel, name='layer', out_shape=(jax.ShapeDtypeStruc...  259 us

profile of v4, /device:TPU:1, one launch (start us, length us, event | category | flops | bytes accessed | tf_op | source)
XLA Modules:
  0.0 263.9 jit_solution(15471840388547667677)
XLA Ops:
  1.3 1.6 tables.1
  2.9 258.7 %layer.1 = (bf16[2048,128]{1,0:T(8,128)(2,1)}, bf16[2048,128]{1,0:T(8,128)(2,1)}, f32[256,128]{1,0:T(8,128)}) custom-call(s32[8,128]{1,0:T(8,128)} %get-tuple-element.9.etab_in, s32[8,128]{1,0:T(8,128)} %get-tuple-element.10.meta_ref, bf16[2048,128]{1,0:T(8,128)(2,1)} %nf_in.1, bf16[2048,128]{1,0:T(8,128)(2,1)} %cot_in.1, bf16[128,128]{1,0:T(8,128)(2,1)} %wm_in.1, ...), custom_call_target="tpu_custom_call" | custom-call | tf_op jit(solution)/shard_map/layer/pallas_call | solution.py:592
  261.6 2.3 store.1

commit v5 on v4

--- a/solution.py
+++ b/solution.py
@@ -16,6 +16,8 @@
 NH = 2
 PIECE = BLK // NH
 NT = NZ * NH
+LEAD = 4
+LAG = 4
 SLAB = NX * NY * 2
 CHUNK = 2 * PEERS
 EDGES = 64
@@ -108,7 +110,7 @@
     none = float(EDGES)
     for row, prev_row, last_row in ((0, SRC_PREV, SRC_LAST), (1, DST_PREV, DST_LAST)):
         slot = pad[0, row : row + 1, :]
-        etab_ref[(SRC, DST)[row] : (SRC, DST)[row] + 1] = slot
+        etab_ref[(SRC, DST)[row] : (SRC, DST)[row] + 1] = (slot // 2) * (2 * NH) + slot % 2
         on = lax.broadcasted_iota(I32, slot.shape, 1) < live
         flat = jnp.where(on, slot.astype(F32), -1.0)
         tall = jnp.sum(jnp.where(down == along, flat, 0.0), axis=1, keepdims=True)
@@ -187,10 +189,13 @@
     loop(0, OWN, project)
     pl.semaphore_wait(barrier, len(peers))
 
-    def slots_of(px, zi, pc):
-        return pl.ds(((px * NZ + zi) * 2 + pc) * 2, 2)
-
-    def gather(forward):
+    def spot_of(px, zi, pc, h):
+        return (((px * NZ + zi) * 2 + pc) * NH + h) * 2
+
+    def spots_of(px, zi, pc, h):
+        return pl.ds(spot_of(px, zi, pc, h), 2)
+
+    def gather(forward, after):
         block_row = SRC if forward else DST
 
         def source_of(t):
@@ -215,7 +220,7 @@
             px, pc = slab_peer(x, c, j)
             zi = source_of(t)
             return remote(
-                staged.at[px * 2 + pc, zi, t % NH], rows.at[slots_of(x, zi, c), t % NH],
+                staged.at[px * 2 + pc, zi, t % NH], rows.at[spots_of(x, zi, c, t % NH)],
                 g_xs.at[t, j], g_xr.at[t, j], device(px, y, z, pc),
             )
 
@@ -267,9 +272,9 @@
                     staged[pid, zi, h, s] = chunk[meta[zi, block_row, CHUNK * z + pid * 2 + s]]
 
             loop(1, PEERS, pick)
-            base = ((x * NZ + zi) * 2 + c) * 2
+            base = spot_of(x, zi, c, h)
             for s in range(2):
-                rows[base + s, h] = chunk[meta[zi, block_row, CHUNK * z + me * 2 + s]]
+                rows[base + s] = chunk[meta[zi, block_row, CHUNK * z + me * 2 + s]]
             loop(1, PEERS, lambda j: xcopy(t, j).start())
 
         for h in range(NH):
@@ -286,6 +291,19 @@
                 for dy in (1, 3, 2):
                     ycopy(h, dy).start()
 
+        def drain(t):
+            zi = source_of(t)
+
+            def each(j):
+                xcopy(t, j).wait_send()
+                sx, sc = slab_source(x, c, j)
+                remote(
+                    staged.at[me, zi, t % NH], rows.at[spots_of(sx, zi, sc, t % NH)],
+                    g_xs.at[t, j], g_xr.at[t, j], here,
+                ).wait_recv()
+
+            loop(1, PEERS, each)
+
         def step(t):
             @pl.when(t < NH * (NZ - 1))
             def _():
@@ -294,7 +312,21 @@
             collect(t)
             deliver(t)
 
-        loop(NH if forward else 0, NH * NZ, step)
+            @pl.when(t >= LAG)
+            def _():
+                drain(t - LAG)
+                if forward:
+
+                    @pl.when(t >= LAG + NH)
+                    def _():
+                        for dy in range(1, NY):
+                            ycopy(t - LAG, dy).wait_send()
+                else:
+                    for dy in range(1, NY):
+                        ycopy(t - LAG, dy).wait_send()
+
+        loop(NH if forward else 0, NT, step)
+        after()
 
         for d in range(1, NZ):
             if forward:
@@ -302,26 +334,12 @@
             for h in range(NH):
                 zcopy(z, h, d, 1).wait_send()
 
-        def finish(t):
-            zi = source_of(t)
-
-            def each(j):
-                xcopy(t, j).wait_send()
-                sx, sc = slab_source(x, c, j)
-                remote(
-                    staged.at[me, zi, t % NH], rows.at[slots_of(sx, zi, sc), t % NH],
-                    g_xs.at[t, j], g_xr.at[t, j], here,
-                ).wait_recv()
-
-            loop(1, PEERS, each)
-
-        loop(0, NH * NZ, finish)
-
-        def sent(t):
+        def rest(t):
+            drain(t)
             for dy in range(1, NY):
                 ycopy(t, dy).wait_send()
 
-        loop(NH if forward else 0, NH * NZ, sent)
+        loop(NT - LAG, NT, rest)
 
     def whole(pieces):
         return pieces.reshape(BLK, pieces.shape[-1])
@@ -335,7 +353,9 @@
             terms = []
             for i in range(GROUP):
                 k = r * GROUP + i
-                terms.append(dot(adj[k], whole(rows[etab[pick, k]]), contract))
+                at = etab[pick, k]
+                block = jnp.concatenate([rows[at + 2 * h] for h in range(NH)], axis=0)
+                terms.append(dot(adj[k], block, contract))
             for i in range(GROUP):
                 k = r * GROUP + i
                 chain[k] = terms[i].reshape(chain.shape[1:]) + chain[etab[prev, k]]
@@ -353,14 +373,14 @@
             zi, h = owner(t), t % NH
             px, pc = slab_peer(x, c, j)
             return remote(
-                parts.at[slots_of(px, zi, pc), h], arrived.at[zi, h, pl.ds(2 * me, 2)],
+                parts.at[spots_of(px, zi, pc, h)], arrived.at[zi, h, pl.ds(2 * me, 2)],
                 s_xs.at[t, j], s_xr.at[t, j], device(px, y, z, pc),
             )
 
         def local(t):
             zi, h = owner(t), t % NH
             return pltpu.make_async_copy(
-                parts.at[slots_of(x, zi, c), h], arrived.at[zi, h, pl.ds(2 * me, 2)], ls.at[t]
+                parts.at[spots_of(x, zi, c, h)], arrived.at[zi, h, pl.ds(2 * me, 2)], ls.at[t]
             )
 
         def ycopy(t, d):
@@ -381,8 +401,9 @@
 
             def each(pid):
                 base = (((pid // 2) * NZ + zi) * 2 + pid % 2) * 2
+                to = spot_of(pid // 2, zi, pid % 2, h)
                 for s in range(2):
-                    parts[base + s, h] = chain[etab[end, base + s], h].astype(BF16)
+                    parts[to + s] = chain[etab[end, base + s], h].astype(BF16)
 
             loop(0, PEERS, each)
 
@@ -396,8 +417,7 @@
             write(t)
             push(t - 1)
 
-        loop(1, NH * NZ, issue)
-        push(NH * NZ - 1)
+        loop(1, LEAD + 1, issue)
 
         runs[CHUNK] = jnp.zeros(runs.shape[1:], F32)
 
@@ -408,7 +428,7 @@
             def each(j):
                 sx, sc = slab_source(x, c, j)
                 remote(
-                    parts.at[slots_of(x, zi, c), h], arrived.at[zi, h, pl.ds(2 * (sx * 2 + sc), 2)],
+                    parts.at[spots_of(x, zi, c, h)], arrived.at[zi, h, pl.ds(2 * (sx * 2 + sc), 2)],
                     s_xs.at[t, j], s_xr.at[t, j], here,
                 ).wait_recv()
 
@@ -441,13 +461,31 @@
                 zsend[d - 1, h, b] = value.astype(BF16)
             zcopy(d, h).start()
 
-        loop(0, NH, merge)
+        def drain(t):
+            for d in range(1, NY):
+                ycopy(t, d).wait_send()
+            loop(1, PEERS, lambda j: xcopy(t, j).wait_send())
 
         def step(t):
             merge(t)
-            pass_on(t - NH)
-
-        loop(NH, NH * NZ, step)
+
+            @pl.when(t < NT - LEAD - 1)
+            def _():
+                write(t + LEAD + 1)
+
+            @pl.when(t < NT - LEAD)
+            def _():
+                push(t + LEAD)
+
+            @pl.when(t >= NH)
+            def _():
+                pass_on(t - NH)
+
+            @pl.when(t >= LAG)
+            def _():
+                drain(t - LAG)
+
+        loop(0, NT, step)
         for h in range(NH):
             for b, value in enumerate(total_of(NH * (NZ - 1) + h)):
                 total[b, h] = value
@@ -461,12 +499,7 @@
             for h in range(NH):
                 zcopy(d, h).wait_send()
 
-        def finish(t):
-            for d in range(1, NY):
-                ycopy(t, d).wait_send()
-            loop(1, PEERS, lambda j: xcopy(t, j).wait_send())
-
-        loop(0, NH * NZ, finish)
+        loop(NT - LAG, NT, drain)
 
     def share(i, d):
         part = (out_ref, gf_ref)[i].at[mine_rows]
@@ -481,7 +514,7 @@
     def block_rows(b):
         return pl.ds(pl.multiple_of((QTR * y + b) * BLK, BLK), BLK)
 
-    gather(True)
+    gather(True, lambda: None)
     for fetch in fetches[2:]:
         fetch.wait()
     edges(True)
@@ -510,10 +543,12 @@
     for b in range(QTR):
         outer(BLK, b, pre[b])
 
-    gather(False)
+    def share_out():
+        for d in (1, 3, 2):
+            share(0, d).start()
+
+    gather(False, share_out)
     edges(False)
-    for d in (1, 3, 2):
-        share(0, d).start()
     scatter(False)
 
     for b in range(QTR):
@@ -611,9 +646,9 @@
             pltpu.VMEM((NZ, NH, OWN, *piece), BF16),
             pltpu.VMEM((OWN, *piece), BF16),
             pltpu.VMEM((PEERS, NZ, NH, 2, *piece), BF16),
-            pltpu.VMEM((SLOTS, NH, *piece), BF16),
+            pltpu.VMEM((SLOTS * NH, *piece), BF16),
             pltpu.VMEM((EDGES + 1, NH, *piece), F32),
-            pltpu.VMEM((SLOTS, NH, *piece), BF16),
+            pltpu.VMEM((SLOTS * NH, *piece), BF16),
             pltpu.VMEM((NZ, NH, CHUNK, *piece), BF16),
             pltpu.VMEM((CHUNK + 1, *piece), F32),
             pltpu.VMEM((NT, NY - 1, QTR, *piece), BF16),

time: 264 us -> 262 us (level)
  no operation moved by 1% of the time
where the time goes in v5:
time: 262 us
  Pallas kernels  261 us (100%)
    pallas_call x1, Pallas kernels, layer(): pl.pallas_call(layer_kernel, name='layer', out_shape=(jax.ShapeDtypeStruc...  257 us

profile of v5, /device:TPU:1, one launch (start us, length us, event | category | flops | bytes accessed | tf_op | source)
XLA Modules:
  0.0 261.8 jit_solution(7348015678669293939)
XLA Ops:
  1.3 1.6 tables.1
  2.9 256.7 %layer.1 = (bf16[2048,128]{1,0:T(8,128)(2,1)}, bf16[2048,128]{1,0:T(8,128)(2,1)}, f32[256,128]{1,0:T(8,128)}) custom-call(s32[8,128]{1,0:T(8,128)} %get-tuple-element.9.etab_in, s32[8,128]{1,0:T(8,128)} %get-tuple-element.10.meta_ref, bf16[2048,128]{1,0:T(8,128)(2,1)} %nf_in.1, bf16[2048,128]{1,0:T(8,128)(2,1)} %cot_in.1, bf16[128,128]{1,0:T(8,128)(2,1)} %wm_in.1, ...), custom_call_target="tpu_custom_call" | custom-call | tf_op jit(solution)/shard_map/layer/pallas_call | solution.py:627
  259.6 2.3 store.1
